TPU v7x, 32 devices: a whole 2x2x4 slice. The times are simulated.
32 devices in a mesh: seq: 8 (over z, core), head: 4 (over y, x).
Axes of the slice: x: 2, y: 2, z: 4, core: 2. Of those that a mesh axis runs over, the one named last changes fastest.
Arguments:
- video_query: bfloat16 [4096, 3072], P(('seq', 'head')), may hold values from -8 to 8
- video_key: bfloat16 [4096, 3072], P(('seq', 'head')), may hold values from -8 to 8
- video_value: bfloat16 [4096, 3072], P(('seq', 'head')), may hold values from -6 to 6
- video_grad: bfloat16 [4096, 3072], P(('seq', 'head')), may hold values from -6 to 6
- text_query: bfloat16 [256, 3072], P(None, 'head'), may hold values from -8 to 8
- text_key: bfloat16 [256, 3072], P(None, 'head'), may hold values from -8 to 8
- text_value: bfloat16 [256, 3072], P(None, 'head'), may hold values from -6 to 6
- text_grad: bfloat16 [256, 3072], P(None, 'head'), may hold values from -6 to 6
- tile_list: int32 [32, 8], replicated, may hold values from 0 to 31, as said below
- tile_count: int32 [32], replicated, may hold values from 1 to 8, as said below
- text_mask: int32 [256], replicated, may hold values from 0 to 1, as said below
Outputs:
- attended_video: bfloat16 [4096, 3072], P(('seq', 'head'))
- video_query_grad: bfloat16 [4096, 3072], P(('seq', 'head'))
- video_key_grad: bfloat16 [4096, 3072], P(('seq', 'head'))
- video_value_grad: bfloat16 [4096, 3072], P(('seq', 'head'))
- attended_text: bfloat16 [256, 3072], P(None, 'head')
- text_query_grad: bfloat16 [256, 3072], P(None, 'head')
- text_key_grad: bfloat16 [256, 3072], P(None, 'head')
- text_value_grad: bfloat16 [256, 3072], P(None, 'head')
Inputs may be any that keep to these rules, and one draw needn't show every extreme that they name: `tile_list`: the 8 entries of one query tile's list are distinct. Query tiles fall in aligned blocks of 4; the used entries of one block together name at most 2 distinct tiles of any other block of 4 tiles, and every block names exactly 2 from some other block. `tile_count`: every aligned block of 4 query tiles has a tile that uses all 8 entries. `text_mask`: the ones form a prefix of at least 64 entries.
All inputs are finite; a program needn't handle non-finite values.
Results may differ from a plain program's by a relative error of at most 0.012.
Values may be sent and summed in bfloat16 or wider, within the bound.
A program may use at most 192 MiB of HBM per device.

v0:
```python
import jax
import jax.numpy as jnp
from jax import lax
from jax.sharding import PartitionSpec as P

HD = 128
TXT = 256
TILE = 128
KT = 8
MOST = 2


NEGATIVE = -1e30
HIGHEST_PRECISION = lax.Precision.HIGHEST


def split_product(form, weights, data):
    upper = weights.astype(jnp.bfloat16)
    lower = (weights - upper.astype(jnp.float32)).astype(jnp.bfloat16)
    return jnp.einsum(form, upper, data, preferred_element_type=jnp.float32) + jnp.einsum(
        form, lower, data, preferred_element_type=jnp.float32
    )


def block_scores(query_blk, key_blk, live_blk, factor):
    scores = (
        jnp.einsum("bthd,bkhd->bhtk", query_blk, key_blk, preferred_element_type=jnp.float32)
        * factor
    )
    scores = jnp.where(live_blk[:, None, None, :], scores, NEGATIVE)
    maximum = jnp.max(scores, axis=-1)
    log_total = maximum + jnp.log(jnp.sum(jnp.exp(scores - maximum[..., None]), axis=-1))
    return (scores, log_total)


def block_forward(scores, log_total, value_blk, grad_blk):
    weights = jnp.exp(scores - log_total[..., None]).astype(jnp.bfloat16)
    output = jnp.einsum("bhtk,bkhd->bthd", weights, value_blk, preferred_element_type=jnp.float32)
    offset = jnp.sum(grad_blk.astype(jnp.float32) * output, axis=-1)
    return (output, jnp.transpose(offset, (0, 2, 1)))


def block_backward(scores, log_total, offset, query_blk, key_blk, value_blk, grad_blk, factor):
    probability = jnp.exp(scores - log_total[..., None])
    weights = probability.astype(jnp.bfloat16)
    prob_grad = jnp.einsum(
        "bthd,bkhd->bhtk", grad_blk, value_blk, preferred_element_type=jnp.float32
    )
    score_grad = (probability * (prob_grad - offset[..., None])).astype(jnp.bfloat16)
    query_grad = (
        jnp.einsum("bhtk,bkhd->bthd", score_grad, key_blk, preferred_element_type=jnp.float32)
        * factor
    )
    key_grad = (
        jnp.einsum("bhtk,bthd->bkhd", score_grad, query_blk, preferred_element_type=jnp.float32)
        * factor
    )
    value_grad = jnp.einsum(
        "bhtk,bthd->bkhd", weights, grad_blk, preferred_element_type=jnp.float32
    )
    return (query_grad, key_grad, value_grad)


def spread_grads(pool_total, text_total, grad_blk, pool_slot):
    block_tiles = grad_blk.shape[0]
    tile_part = grad_blk[:, : KT * TILE].reshape(block_tiles, KT, TILE, pool_total.shape[2])
    return (
        pool_total.at[pool_slot].add(tile_part),
        text_total + jnp.sum(grad_blk[:, KT * TILE :], axis=0),
    )


def body(
    video_query,
    video_key,
    video_value,
    video_grad,
    text_query,
    text_key,
    text_value,
    text_grad,
    tile_list,
    tile_count,
    text_mask,
):
    factor = HD ** (-0.5)
    groups = lax.axis_size("seq")
    own_group = lax.axis_index("seq")
    query_rows, key_rows, value_rows, grad_rows = (
        lax.all_to_all(video_query, "head", split_axis=1, concat_axis=0, tiled=True),
        lax.all_to_all(video_key, "head", split_axis=1, concat_axis=0, tiled=True),
        lax.all_to_all(video_value, "head", split_axis=1, concat_axis=0, tiled=True),
        lax.all_to_all(video_grad, "head", split_axis=1, concat_axis=0, tiled=True),
    )
    token_rows, feature_width = query_rows.shape
    head_count = feature_width // HD
    shard_tiles = token_rows // TILE
    tile_total = tile_list.shape[0]
    text_ok = text_mask > 0
    entry_live = jnp.arange(KT)[None, :] < tile_count[:, None]
    tile_hits = (tile_list[:, :, None] == jnp.arange(tile_total)[None, None, :]) & entry_live[
        :, :, None
    ]
    wanted = jnp.any(
        jnp.any(tile_hits, axis=1).reshape(groups, shard_tiles, tile_total), axis=1
    ).reshape(groups, groups, shard_tiles)
    slot_rank = jnp.cumsum(wanted.astype(jnp.int32), axis=2) - 1
    distinct = (jnp.arange(groups)[:, None] != jnp.arange(groups)[None, :])[:, :, None, None]
    select = (
        wanted[:, :, None, :]
        & (slot_rank[:, :, None, :] == jnp.arange(MOST)[None, None, :, None])
        & distinct
    )
    outgoing = lax.dynamic_index_in_dim(select, own_group, 1, keepdims=False)
    incoming = lax.dynamic_index_in_dim(select, own_group, 0, keepdims=False)
    picker = outgoing.reshape(groups * MOST, shard_tiles).astype(jnp.bfloat16)
    send_keys = jnp.dot(
        picker,
        key_rows.reshape(shard_tiles, TILE * feature_width),
        preferred_element_type=jnp.float32,
    )
    send_keys = send_keys.astype(jnp.bfloat16).reshape(groups, MOST * TILE, feature_width)
    send_values = jnp.dot(
        picker,
        value_rows.reshape(shard_tiles, TILE * feature_width),
        preferred_element_type=jnp.float32,
    )
    send_values = send_values.astype(jnp.bfloat16).reshape(groups, MOST * TILE, feature_width)
    owner_base = (
        jnp.arange(groups, dtype=jnp.int32)[:, None, None] * shard_tiles
        + jnp.arange(shard_tiles, dtype=jnp.int32)[None, None, :]
    )
    slot_ids = jnp.where(
        jnp.any(incoming, axis=2), jnp.sum(jnp.where(incoming, owner_base, 0), axis=2), -1
    ).reshape(groups * MOST)
    pool_ids = jnp.concatenate(
        [own_group * shard_tiles + jnp.arange(shard_tiles, dtype=jnp.int32), slot_ids]
    )
    pool_size = shard_tiles + groups * MOST
    my_list = lax.dynamic_slice_in_dim(tile_list, own_group * shard_tiles, shard_tiles, 0)
    my_count = lax.dynamic_slice_in_dim(tile_count, own_group * shard_tiles, shard_tiles, 0)
    pool_match = my_list[:, :, None] == pool_ids[None, None, :]
    pool_slot = jnp.sum(jnp.where(pool_match, jnp.arange(pool_size, dtype=jnp.int32), 0), axis=2)
    live_entry = jnp.any(pool_match, axis=2) & (jnp.arange(KT)[None, :] < my_count[:, None])
    text_query3 = text_query.reshape(TXT, head_count, HD)
    text_key3 = text_key.reshape(TXT, head_count, HD)
    text_value3 = text_value.reshape(TXT, head_count, HD)
    text_grad3 = text_grad.reshape(TXT, head_count, HD)
    block_tiles = min(shard_tiles, max(1, 512 // TILE))
    block_count = shard_tiles // block_tiles
    query_blocks = query_rows.reshape(block_count, block_tiles, TILE, head_count, HD)
    grad_blocks = grad_rows.reshape(block_count, block_tiles, TILE, head_count, HD)
    slot_blocks = pool_slot.reshape(block_count, block_tiles, KT)
    live_blocks = jnp.concatenate(
        [
            jnp.repeat(live_entry, TILE, axis=1),
            jnp.broadcast_to(text_ok[None, :], (shard_tiles, TXT)),
        ],
        axis=1,
    )
    live_blocks = live_blocks.reshape(block_count, block_tiles, KT * TILE + TXT)
    local_keys = key_rows.reshape(shard_tiles, TILE, feature_width)
    local_values = value_rows.reshape(shard_tiles, TILE, feature_width)

    def build_pool(received):
        got_keys, got_values = received
        return (
            jnp.concatenate(
                [local_keys, got_keys.reshape(groups * MOST, TILE, feature_width)], axis=0
            ),
            jnp.concatenate(
                [local_values, got_values.reshape(groups * MOST, TILE, feature_width)], axis=0
            ),
        )

    def block_rows(pool, slot_blk, text_part):
        picked = pool[slot_blk].reshape(block_tiles, KT * TILE, head_count, HD)
        return jnp.concatenate(
            [picked, jnp.broadcast_to(text_part[None], (block_tiles, TXT, head_count, HD))], axis=1
        )

    pool_keys, pool_values = build_pool(
        (
            lax.all_to_all(send_keys, "seq", split_axis=0, concat_axis=0, tiled=True),
            lax.all_to_all(send_values, "seq", split_axis=0, concat_axis=0, tiled=True),
        )
    )
    start = (
        jnp.zeros((pool_size, TILE, feature_width), jnp.float32),
        jnp.zeros((pool_size, TILE, feature_width), jnp.float32),
        jnp.zeros((TXT, head_count, HD), jnp.float32),
        jnp.zeros((TXT, head_count, HD), jnp.float32),
    )

    def forward_step(running, inputs):
        query_blk, grad_blk, slot_blk, live_blk = inputs
        key_blk = block_rows(pool_keys, slot_blk, text_key3)
        value_blk = block_rows(pool_values, slot_blk, text_value3)
        scores, log_total = block_scores(query_blk, key_blk, live_blk, factor)
        output, offset = block_forward(scores, log_total, value_blk, grad_blk)
        return (running, (output.astype(jnp.bfloat16), log_total, offset))

    unused, forwards = lax.scan(
        forward_step, None, (query_blocks, grad_blocks, slot_blocks, live_blocks)
    )
    attended_blocks, total_blocks, offset_blocks = forwards
    again_keys, again_values = build_pool(
        (
            lax.all_to_all(send_keys, "seq", split_axis=0, concat_axis=0, tiled=True),
            lax.all_to_all(send_values, "seq", split_axis=0, concat_axis=0, tiled=True),
        )
    )

    def backward_step(running, inputs):
        key_acc, value_acc, text_key_acc, text_value_acc = running
        query_blk, grad_blk, slot_blk, live_blk, log_total, offset = inputs
        key_blk = block_rows(again_keys, slot_blk, text_key3)
        value_blk = block_rows(again_values, slot_blk, text_value3)
        scores, unused_total = block_scores(query_blk, key_blk, live_blk, factor)
        query_grad, key_grad, value_grad = block_backward(
            scores, log_total, offset, query_blk, key_blk, value_blk, grad_blk, factor
        )
        key_acc, text_key_acc = spread_grads(key_acc, text_key_acc, key_grad, slot_blk)
        value_acc, text_value_acc = spread_grads(value_acc, text_value_acc, value_grad, slot_blk)
        return ((key_acc, value_acc, text_key_acc, text_value_acc), query_grad.astype(jnp.bfloat16))

    finals, query_grad_blocks = lax.scan(
        backward_step,
        start,
        (query_blocks, grad_blocks, slot_blocks, live_blocks, total_blocks, offset_blocks),
    )
    key_acc, value_acc, text_key_acc, text_value_acc = finals
    back_keys, back_values = (
        lax.all_to_all(
            key_acc[shard_tiles:].reshape(groups, MOST * TILE, feature_width),
            "seq",
            split_axis=0,
            concat_axis=0,
            tiled=True,
        ),
        lax.all_to_all(
            value_acc[shard_tiles:].reshape(groups, MOST * TILE, feature_width),
            "seq",
            split_axis=0,
            concat_axis=0,
            tiled=True,
        ),
    )
    out_flat = outgoing.reshape(groups * MOST, shard_tiles)
    target_tile = jnp.where(
        jnp.any(out_flat, axis=1),
        jnp.sum(jnp.where(out_flat, jnp.arange(shard_tiles, dtype=jnp.int32)[None, :], 0), axis=1),
        shard_tiles,
    )
    own_key_grad = (
        key_acc[:shard_tiles]
        .at[target_tile]
        .add(back_keys.reshape(groups * MOST, TILE, feature_width), mode="drop")
    )
    own_value_grad = (
        value_acc[:shard_tiles]
        .at[target_tile]
        .add(back_values.reshape(groups * MOST, TILE, feature_width), mode="drop")
    )
    key_rows3 = key_rows.reshape(token_rows, head_count, HD)
    value_rows3 = value_rows.reshape(token_rows, head_count, HD)
    text_query32 = text_query3.astype(jnp.float32)
    text_key32 = text_key3.astype(jnp.float32)
    text_value32 = text_value3.astype(jnp.float32)
    text_grad32 = text_grad3.astype(jnp.float32)
    video_scores = (
        jnp.einsum("thd,khd->htk", text_query3, key_rows3, preferred_element_type=jnp.float32)
        * factor
    )
    text_scores = (
        jnp.einsum("thd,khd->htk", text_query3, text_key3, preferred_element_type=jnp.float32)
        * factor
    )
    text_scores = jnp.where(text_ok[None, None, :], text_scores, NEGATIVE)
    maximum = jnp.maximum(
        lax.pmax(jnp.max(video_scores, axis=-1), "seq"), jnp.max(text_scores, axis=-1)
    )
    video_exp = jnp.exp(video_scores - maximum[..., None])
    denominator, numerator = lax.psum(
        (jnp.sum(video_exp, axis=-1), split_product("htk,khd->thd", video_exp, value_rows3)), "seq"
    )
    text_exp = jnp.exp(text_scores - maximum[..., None])
    denominator = denominator + jnp.sum(text_exp, axis=-1)
    numerator = numerator + jnp.einsum(
        "htk,khd->thd", text_exp, text_value32, precision=HIGHEST_PRECISION
    )
    log_total = maximum + jnp.log(denominator)
    text_out = numerator / denominator.T[:, :, None]
    video_prob = jnp.exp(video_scores - log_total[..., None])
    text_prob = jnp.exp(text_scores - log_total[..., None])
    text_offset = jnp.sum(text_grad32 * text_out, axis=-1).T
    video_dscore = video_prob * (
        jnp.einsum("thd,khd->htk", text_grad3, value_rows3, preferred_element_type=jnp.float32)
        - text_offset[..., None]
    )
    text_dscore = text_prob * (
        jnp.einsum("thd,khd->htk", text_grad3, text_value3, preferred_element_type=jnp.float32)
        - text_offset[..., None]
    )
    query_part = split_product("htk,khd->thd", video_dscore, key_rows3) * factor
    video_key_from_text = split_product("htk,thd->khd", video_dscore, text_query3) * factor
    video_value_from_text = split_product("htk,thd->khd", video_prob, text_grad3)
    query_sum, key_sum, value_sum = lax.psum((query_part, text_key_acc, text_value_acc), "seq")
    text_query_grad = (
        query_sum
        + jnp.einsum("htk,khd->thd", text_dscore, text_key32, precision=HIGHEST_PRECISION) * factor
    )
    text_key_grad = (
        key_sum
        + jnp.einsum("htk,thd->khd", text_dscore, text_query32, precision=HIGHEST_PRECISION)
        * factor
    )
    text_value_grad = value_sum + jnp.einsum(
        "htk,thd->khd", text_prob, text_grad32, precision=HIGHEST_PRECISION
    )
    attended_rows = attended_blocks.reshape(token_rows, feature_width)
    query_grad_rows = query_grad_blocks.reshape(token_rows, feature_width)
    key_grad_rows = (
        own_key_grad.reshape(token_rows, feature_width)
        + video_key_from_text.reshape(token_rows, feature_width)
    ).astype(jnp.bfloat16)
    value_grad_rows = (
        own_value_grad.reshape(token_rows, feature_width)
        + video_value_from_text.reshape(token_rows, feature_width)
    ).astype(jnp.bfloat16)
    attended_video, video_query_grad, video_key_grad, video_value_grad = (
        lax.all_to_all(attended_rows, "head", split_axis=0, concat_axis=1, tiled=True),
        lax.all_to_all(query_grad_rows, "head", split_axis=0, concat_axis=1, tiled=True),
        lax.all_to_all(key_grad_rows, "head", split_axis=0, concat_axis=1, tiled=True),
        lax.all_to_all(value_grad_rows, "head", split_axis=0, concat_axis=1, tiled=True),
    )
    return (
        attended_video,
        video_query_grad,
        video_key_grad,
        video_value_grad,
        text_out.reshape(TXT, feature_width).astype(jnp.bfloat16),
        text_query_grad.reshape(TXT, feature_width).astype(jnp.bfloat16),
        text_key_grad.reshape(TXT, feature_width).astype(jnp.bfloat16),
        text_value_grad.reshape(TXT, feature_width).astype(jnp.bfloat16),
    )


def solution(mesh):
    placed = (
        P(("seq", "head"), None),
        P(("seq", "head"), None),
        P(("seq", "head"), None),
        P(("seq", "head"), None),
        P(None, "head"),
        P(None, "head"),
        P(None, "head"),
        P(None, "head"),
        P(),
        P(),
        P(),
    )
    return jax.shard_map(
        body,
        mesh=mesh,
        in_specs=placed,
        out_specs=(
            P(("seq", "head"), None),
            P(("seq", "head"), None),
            P(("seq", "head"), None),
            P(("seq", "head"), None),
            P(None, "head"),
            P(None, "head"),
            P(None, "head"),
            P(None, "head"),
        ),
        check_vma=False,
    )
```

profile of v0, /device:TPU:0, one launch (start us, length us, event | category | flops | bytes accessed | tf_op | source)
XLA Modules:
  0.0 900.4 jit_solution(9937720170638479781)
XLA Ops:
  9.9 5.2 all-to-all-start
  17.2 8.8 all-to-all-done
  26.0 4.2 all-to-all-start.2
  33.0 2.6 reshape.323
  35.6 4.9 all-to-all-done.2
  40.6 4.9 all-to-all-start.1
  48.2 2.6 reshape.328
  50.8 66.3 %all-to-all-done.1 = bf16[8,256,768]{2,1,0:T(8,128)(2,1)} async-done(((bf16[8,256,768]{2,1,0:T(8,128)(2,1)}), bf16[8,256,768]{2,1,0:T(8,128)(2,1)}, u32[]{:S(2)}, u32[]{:S(2)}) %all-to-all-start.1) | async-done | bytes 3145760 | tf_op jit(solution)/shard_map/all_to_all | solution.py:185
  117.1 3.6 all-to-all-start.3
  122.2 2.3 copy.387
  124.7 67.4 %all-to-all-done.3 = bf16[8,256,768]{2,1,0:T(8,128)(2,1)S(1)} async-done(((bf16[8,256,768]{2,1,0:T(8,128)(2,1)}), bf16[8,256,768]{2,1,0:T(8,128)(2,1)S(1)}, u32[]{:S(2)}, u32[]{:S(2)}) %all-to-all-start.3) | async-done | bytes 3145760 | tf_op jit(solution)/shard_map/all_to_all | solution.py:184
  192.2 4.5 all-to-all-start.4
  200.8 2.3 copy.494
  203.1 3.3 pad_maximum_fusion.7
  206.4 5.8 gather_fusion.1
  212.2 13.7 %reshape.401 = bf16[4,1024,6,128]{3,2,1,0:T(8,128)(2,1)} reshape(bf16[32,128,768]{2,1,0:T(8,128)(2,1)} %gather_fusion.1) | data formatting | bytes 12582912 | tf_op jit(solution)/shard_map/while/body/eval_jaxpr/reshape | solution.py:177
  225.9 7.5 copy.386
  233.3 4.1 pad_maximum_fusion.6
  237.4 5.8 gather_fusion
  243.2 13.7 %reshape.400 = bf16[4,1024,6,128]{3,2,1,0:T(8,128)(2,1)} reshape(bf16[32,128,768]{2,1,0:T(8,128)(2,1)} %gather_fusion) | data formatting | bytes 12582912 | tf_op jit(solution)/shard_map/while/body/eval_jaxpr/reshape | solution.py:177
  256.9 11.5 %copy.380 = bf16[4,1024,6,128]{1,3,2,0:T(8,128)(2,1)} copy(bf16[4,1024,6,128]{3,2,1,0:T(8,128)(2,1)} %reshape.400) | data formatting | bytes 12582912 | tf_op jit(solution)/shard_map/while/body/eval_jaxpr/reshape | solution.py:177
  268.4 4.2 all-to-all-start.6
  272.9 5.9 bitcast_reduce_fusion
  278.9 3.5 fusion.2
  285.7 10.6 %bitcast_convert_fusion = (bf16[4,128,6,128]{1,3,2,0:T(8,128)(2,1)}, f32[4,6,128,128]{3,2,1,0:T(8,128)S(1)}) fusion(f32[4,6,1280,128]{3,2,1,0:T(8,128)} %copy-done.2, f32[4,6,128]{2,1,0:T(8,128)S(1)} %log_add_fusion, pred[4,1280]{1,0:T(4,128)(4,1)S(1)} %pad_add_fusion, bf16[4,256,6,128]{1,3,2,0:T(8,128)(2,1)S(1)} %broadcast_in_dim.182, ...), kind=kOutput, calls=%fused_computation.44 | convolution fusion | flops 1038483456 | bytes 25969664 | tf_op jit(solution)/shard_map/while/body/eval_jaxpr/bhtk,bkhd->bthd/dot_general | solution.py:38
  296.3 4.7 all-to-all-start.5
  301.3 13.0 %fusion = bf16[4,6,128,1280]{2,3,1,0:T(8,128)(2,1)} fusion(f32[4,6,1280,128]{3,2,1,0:T(8,128)} %copy-done.2, bf16[4,128,6,128]{1,3,2,0:T(8,128)(2,1)S(1)} %bitcast.180, f32[4,6,128]{2,1,0:T(8,128)S(1)} %bitcast.208, f32[4,6,128]{2,1,0:T(8,128)S(1)} %log_add_fusion, pred[4,1280]{1,0:T(4,128)(4,1)S(1)} %pad_add_fusion, ...), kind=kOutput, calls=%fused_computation.9 | convolution fusion | flops 1045954560 | bytes 32273408 | tf_op jit(solution)/shard_map/while/body/eval_jaxpr/bthd,bkhd->bhtk/dot_general | solution.py:46
  314.3 8.4 multiply_convert_fusion
  322.7 4.4 all-to-all-start.7
  327.0 11.1 %convolution_bitcast_fusion = f32[4,1280,6,128]{3,1,2,0:T(8,128)} fusion(bf16[4,128,6,128]{1,3,2,0:T(8,128)(2,1)S(1)} %bitcast.181, f32[4,6,1280,128]{3,2,1,0:T(8,128)} %copy-done.2, f32[4,6,128]{2,1,0:T(8,128)S(1)} %log_add_fusion, pred[4,1280]{1,0:T(4,128)(4,1)S(1)} %pad_add_fusion), kind=kOutput, calls=%fused_computation.19 | convolution fusion | flops 1022361600 | bytes 32261120 | tf_op jit(solution)/shard_map/while/body/eval_jaxpr/bhtk,bthd->bkhd/dot_general | solution.py:58
  338.1 10.4 %slice.43 = f32[4,1024,6,128]{3,1,2,0:T(8,128)} slice(f32[4,1280,6,128]{3,1,2,0:T(8,128)} %convolution_bitcast_fusion), slice={[0:4], [0:1024], [0:6], [0:128]} | slice | bytes 25165824 | tf_op jit(solution)/shard_map/while/body/eval_jaxpr/slice | solution.py:66
  348.5 17.8 %copy.498 = f32[4,1024,6,128]{3,2,1,0:T(8,128)} copy(f32[4,1024,6,128]{3,1,2,0:T(8,128)} %slice.43) | data formatting | bytes 25165824 | tf_op jit(solution)/shard_map/while/body/eval_jaxpr/reshape | solution.py:66
  366.3 16.1 %reshape.404 = f32[32,128,768]{2,1,0:T(8,128)} reshape(f32[4,1024,6,128]{3,2,1,0:T(8,128)} %copy.498) | data formatting | bytes 25165824 | tf_op jit(solution)/shard_map/while/body/eval_jaxpr/reshape | solution.py:66
  382.4 4.0 broadcast.165.clone.1
  386.4 30.1 %scatter_fusion.2 = f32[20,128,768]{2,1,0:T(8,128)} fusion(f32[20,128,768]{2,1,0:T(8,128)} %broadcast.165.clone.1, s32[32]{0:T(128)S(1)} %reshape.345, f32[32,128,768]{2,1,0:T(8,128)} %reshape.404), kind=kCustom, calls=%fused_computation.4 | custom fusion | flops 3145728 | bytes 37748864 | tf_op jit(solution)/shard_map/while/body/eval_jaxpr/scatter-add | solution.py:68
  416.4 6.2 slice.45
  423.5 4.7 all-to-all-start.10
  428.2 11.1 %multiply_bitcast_fusion = f32[4,1280,6,128]{3,1,2,0:T(8,128)} fusion(bf16[4,6,128,1280]{2,3,1,0:T(8,128)(2,1)} %fusion, bf16[4,128,6,128]{1,3,2,0:T(8,128)(2,1)} %bitcast.14), kind=kOutput, calls=%fused_computation.16 | convolution fusion | flops 1010565120 | bytes 24379392 | tf_op jit(solution)/shard_map/while/body/eval_jaxpr/bhtk,bthd->bkhd/dot_general | solution.py:55
  439.4 10.4 %slice.40 = f32[4,1024,6,128]{3,1,2,0:T(8,128)} slice(f32[4,1280,6,128]{3,1,2,0:T(8,128)} %multiply_bitcast_fusion), slice={[0:4], [0:1024], [0:6], [0:128]} | slice | bytes 25165824 | tf_op jit(solution)/shard_map/while/body/eval_jaxpr/slice | solution.py:66
  449.7 17.8 %copy.496 = f32[4,1024,6,128]{3,2,1,0:T(8,128)} copy(f32[4,1024,6,128]{3,1,2,0:T(8,128)} %slice.40) | data formatting | bytes 25165824 | tf_op jit(solution)/shard_map/while/body/eval_jaxpr/reshape | solution.py:66
  467.6 16.3 %reshape.402 = f32[32,128,768]{2,1,0:T(8,128)} reshape(f32[4,1024,6,128]{3,2,1,0:T(8,128)} %copy.496) | data formatting | bytes 25165824 | tf_op jit(solution)/shard_map/while/body/eval_jaxpr/reshape | solution.py:66
  483.9 3.9 broadcast.165.clone
  487.9 30.2 %scatter_fusion = f32[20,128,768]{2,1,0:T(8,128)} fusion(f32[20,128,768]{2,1,0:T(8,128)} %broadcast.165.clone, s32[32]{0:T(128)S(1)} %reshape.345, f32[32,128,768]{2,1,0:T(8,128)} %reshape.402), kind=kCustom, calls=%fused_computation.2 | custom fusion | flops 3145728 | bytes 37748864 | tf_op jit(solution)/shard_map/while/body/eval_jaxpr/scatter-add | solution.py:68
  518.0 6.0 slice.42
  524.1 43.1 %all-to-all-done.10 = f32[8,256,768]{2,1,0:T(8,128)} async-done(((f32[8,256,768]{2,1,0:T(8,128)}), f32[8,256,768]{2,1,0:T(8,128)}, u32[]{:S(2)}, u32[]{:S(2)}) %all-to-all-start.10) | async-done | bytes 6291488 | tf_op jit(solution)/shard_map/all_to_all | solution.py:241
  567.2 4.9 all-to-all-start.8
  583.3 103.5 %pmax.7 = f32[6,256]{1,0:T(8,128)} all-reduce(f32[6,256]{1,0:T(8,128)S(1)} %get-tuple-element.153), channel_id=1, replica_groups=mesh['seq'=8,'head'=4] {'seq'}, use_global_device_ids=true, to_apply=%region_12.13 | all-reduce | flops 1536 | bytes 12288 | tf_op jit(solution)/shard_map/pmax | solution.py:281
  692.3 44.6 %psum.35 = f32[6,256]{1,0:T(8,128)} all-reduce(f32[6,256]{1,0:T(8,128)S(1)} %fusion.9), channel_id=1, replica_groups=mesh['seq'=8,'head'=4] {'seq'}, use_global_device_ids=true, to_apply=%region_15.16 | all-reduce | flops 1536 | bytes 12288 | tf_op jit(solution)/shard_map/psum | solution.py:284
  744.6 2.7 reshape.405
  747.3 32.3 %all-reduce.4.cloned.1.call-done = f32[256,6,128]{2,0,1:T(8,128)} async-done(((f32[256,6,128]{2,0,1:T(8,128)}), f32[256,6,128]{2,0,1:T(8,128)}) %all-reduce.4.cloned.1.call-update) | async-done | bytes 786448 | tf_op jit(solution)/shard_map/psum | solution.py:284
  779.6 4.3 fusion.70
  793.7 3.2 slice_reduce_fusion.1
  797.0 3.4 multiply_bitcast_fusion.1
  802.4 3.8 copy.497
  806.2 2.6 reshape.403
  812.1 9.2 %scatter_fusion.3 = f32[4,128,768]{2,1,0:T(8,128)S(1)} fusion(f32[4,128,768]{2,1,0:T(8,128)S(1)} %slice_add_fusion, s32[16]{0:T(128)S(1)} %copy-done.35, f32[16,128,768]{2,1,0:T(8,128)} %bitcast.47), kind=kCustom, calls=%fused_computation.5 | custom fusion | flops 1572864 | bytes 18874432 | tf_op jit(solution)/shard_map/scatter-add | solution.py:263
  822.4 4.4 all-to-all-start.11
  828.9 2.3 copy.493
  831.2 2.3 copy.495
  833.5 29.9 %all-reduce.6.cloned.1.call-done = (f32[256,6,128]{2,0,1:T(8,128)}, f32[256,6,128]{2,0,1:T(8,128)}, f32[256,6,128]{0,2,1:T(8,128)}) async-done(((f32[256,6,128]{2,0,1:T(8,128)}, f32[256,6,128]{2,0,1:T(8,128)}, f32[256,6,128]{0,2,1:T(8,128)}), (f32[256,6,128]{2,0,1:T(8,128)}, f32[256,6,128]{2,0,1:T(8,128)}, f32[256,6,128]{0,2,1:T(8,128)})) %all-reduce.6.cloned.1.call-update) | async-done | bytes 2359312 | tf_op jit(solution)/shard_map/psum | solution.py:308
  863.4 3.0 fusion.38
  868.3 9.1 %scatter_fusion.1 = f32[4,128,768]{2,1,0:T(8,128)S(1)} fusion(f32[4,128,768]{2,1,0:T(8,128)S(1)} %slice_add_fusion.1, s32[16]{0:T(128)S(1)} %copy-done.35, f32[16,128,768]{2,1,0:T(8,128)} %bitcast.41), kind=kCustom, calls=%fused_computation.3 | custom fusion | flops 1572864 | bytes 18874432 | tf_op jit(solution)/shard_map/scatter-add | solution.py:258
  878.4 3.8 all-to-all-start.9
  885.3 2.6 fusion.39
  (188 shorter events, 74.5 us)
Async XLA Ops:
  7.2 8.0 copy-start.33
  7.2 8.0 copy-start.38
  7.2 8.4 copy-start.26
  9.9 16.0 %all-to-all-start = ((bf16[128,4,768]{2,0,1:T(8,128)(2,1)}), bf16[128,4,768]{2,0,1:T(8,128)(2,1)S(1)}, u32[]{:S(2)}, u32[]{:S(2)}) async-start(bf16[128,4,768]{2,0,1:T(8,128)(2,1)} %copy.369), calls=%async_computation | async-start | bytes 1572864 | tf_op jit(solution)/shard_map/all_to_all | solution.py:92
  26.0 6.1 copy-start.11
  26.0 14.6 %all-to-all-start.2 = ((bf16[128,4,768]{2,0,1:T(8,128)(2,1)}), bf16[128,4,768]{2,0,1:T(8,128)(2,1)}, u32[]{:S(2)}, u32[]{:S(2)}) async-start(bf16[128,4,768]{2,0,1:T(8,128)(2,1)} %copy.382), calls=%async_computation.2 | async-start | bytes 1572864 | tf_op jit(solution)/shard_map/all_to_all | solution.py:91
  30.4 91.1 %copy-start.29 = (pred[8,8,2,4]{1,3,2,0:T(4,128)(4,1)}, pred[8,8,2,4]{1,3,2,0:T(4,128)(4,1)S(1)}, u32[]{:S(2)}) copy-start(pred[8,8,2,4]{1,3,2,0:T(4,128)(4,1)S(1)} %fusion.48) | copy-start | bytes 1540
  40.6 76.5 %all-to-all-start.1 = ((bf16[8,256,768]{2,1,0:T(8,128)(2,1)}), bf16[8,256,768]{2,1,0:T(8,128)(2,1)}, u32[]{:S(2)}, u32[]{:S(2)}) async-start(bf16[8,256,768]{2,1,0:T(8,128)(2,1)} %reshape.323), calls=%async_computation.1 | async-start | bytes 6291456 | tf_op jit(solution)/shard_map/all_to_all | solution.py:185
  50.8 70.0 %copy-start.39 = (s32[256]{0:T(256)S(1)}, s32[256]{0:T(256)}, u32[]{:S(2)}) copy-start(s32[256]{0:T(256)} %param.21) | copy-start | bytes 3076
  117.1 75.1 %all-to-all-start.3 = ((bf16[8,256,768]{2,1,0:T(8,128)(2,1)}), bf16[8,256,768]{2,1,0:T(8,128)(2,1)S(1)}, u32[]{:S(2)}, u32[]{:S(2)}) async-start(bf16[8,256,768]{2,1,0:T(8,128)(2,1)} %reshape.328), calls=%async_computation.3 | async-start | bytes 6291456 | tf_op jit(solution)/shard_map/all_to_all | solution.py:184
  120.8 0.5 copy-start.36
  192.2 76.2 %all-to-all-start.4 = ((bf16[128,4,768]{0,2,1:T(8,128)(2,1)}), bf16[128,4,768]{0,2,1:T(8,128)(2,1)}, u32[]{:S(2)}, u32[]{:S(2)}) async-start(bf16[128,4,768]{0,2,1:T(8,128)(2,1)} %bitcast.192), calls=%async_computation.4 | async-start | bytes 1572864 | tf_op jit(solution)/shard_map/all_to_all | solution.py:90
  197.9 8.5 copy-start.15
  225.9 7.5 copy-start.12
  256.9 15.7 %copy-start.25 = (bf16[256,6,128]{2,0,1:T(8,128)(2,1)S(1)}, bf16[256,6,128]{2,0,1:T(8,128)(2,1)}, u32[]{:S(2)}) copy-start(bf16[256,6,128]{2,0,1:T(8,128)(2,1)} %copy.385) | copy-start | bytes 1179652
  268.4 27.9 %all-to-all-start.6 = ((bf16[128,4,768]{0,2,1:T(8,128)(2,1)}), bf16[128,4,768]{0,2,1:T(8,128)(2,1)S(1)}, u32[]{:S(2)}, u32[]{:S(2)}) async-start(bf16[128,4,768]{0,2,1:T(8,128)(2,1)} %bitcast.20), calls=%async_computation.6 | async-start | bytes 1572864 | tf_op jit(solution)/shard_map/all_to_all | solution.py:93
  272.9 5.9 copy-start.22
  278.8 5.5 copy-start.2
  278.8 5.5 copy-start.18
  284.5 1.2 copy-start.24
  296.3 26.3 %all-to-all-start.5 = ((bf16[4,128,768]{1,2,0:T(8,128)(2,1)}), bf16[4,128,768]{1,2,0:T(8,128)(2,1)S(1)}, u32[]{:S(2)}, u32[]{:S(2)}) async-start(bf16[4,128,768]{1,2,0:T(8,128)(2,1)} %bitcast.203), calls=%async_computation.5 | async-start | bytes 1572864 | tf_op jit(solution)/shard_map/all_to_all | solution.py:332
  301.3 13.0 %copy-start.23 = (bf16[4,256,6,128]{3,1,2,0:T(8,128)(2,1)S(1)}, bf16[4,256,6,128]{3,1,2,0:T(8,128)(2,1)}, u32[]{:S(2)}) copy-start(bf16[4,256,6,128]{3,1,2,0:T(8,128)(2,1)} %copy-done.22) | copy-start | bytes 4718596
  322.7 15.4 %copy-start.20 = (bf16[4,128,768]{1,2,0:T(8,128)(2,1)}, bf16[4,128,768]{1,2,0:T(8,128)(2,1)S(1)}, u32[]{:S(2)}) copy-start(bf16[4,128,768]{1,2,0:T(8,128)(2,1)S(1)} %all-to-all-done.5) | copy-start | bytes 2359300
  322.7 99.9 %all-to-all-start.7 = ((bf16[4,128,768]{1,2,0:T(8,128)(2,1)}), bf16[4,128,768]{1,2,0:T(8,128)(2,1)S(1)}, u32[]{:S(2)}, u32[]{:S(2)}) async-start(bf16[4,128,768]{1,2,0:T(8,128)(2,1)} %bitcast.202), calls=%async_computation.7 | async-start | bytes 1572864 | tf_op jit(solution)/shard_map/all_to_all | solution.py:333
  422.6 0.9 copy-start.21
  423.5 143.7 %all-to-all-start.10 = ((f32[8,256,768]{2,1,0:T(8,128)}), f32[8,256,768]{2,1,0:T(8,128)}, u32[]{:S(2)}, u32[]{:S(2)}) async-start(f32[8,256,768]{2,1,0:T(8,128)} %bitcast.163), calls=%async_computation.10 | async-start | bytes 12582912 | tf_op jit(solution)/shard_map/all_to_all | solution.py:241
  567.2 5.0 copy-start.30
  567.2 5.5 copy-start.34
  567.2 5.6 copy-start.27
  567.2 5.8 copy-start.28
  567.2 7.4 copy-start.16
  567.2 7.4 copy-start.37
  567.2 255.2 %all-to-all-start.8 = ((f32[8,256,768]{2,1,0:T(8,128)}), f32[8,256,768]{2,1,0:T(8,128)}, u32[]{:S(2)}, u32[]{:S(2)}) async-start(f32[8,256,768]{2,1,0:T(8,128)} %bitcast.162), calls=%async_computation.8 | async-start | bytes 12582912 | tf_op jit(solution)/shard_map/all_to_all | solution.py:234
  572.2 207.5 %all-reduce.4.cloned.1.call-start = ((), (), s32[]{:S(2)}) async-start(), calls=%async_computation.12 | async-start | bytes 1572864 | tf_op jit(solution)/shard_map/psum | solution.py:284
  572.8 5.6 copy-start.13
  573.0 6.0 copy-start.4
  686.8 2.7 copy-start.8
  691.3 172.1 %all-reduce.6.cloned.1.call-start = ((), (), s32[]{:S(2)}) async-start(), calls=%async_computation.13 | async-start | bytes 4718592 | tf_op jit(solution)/shard_map/psum | solution.py:308
  779.6 4.9 copy-start.9
  784.0 0.6 copy-start.31
  784.6 1.3 copy-start.10
  785.8 3.1 copy-start
  785.8 1.3 copy-start.5
  793.7 3.2 copy-start.1
  802.4 6.4 copy-start.3
  802.4 6.4 copy-start.19
  802.4 6.5 copy-start.32
  808.9 1.6 copy-start.14
  810.5 1.6 copy-start.35
  822.4 56.1 %all-to-all-start.11 = ((bf16[4,128,768]{2,1,0:T(8,128)(2,1)}), bf16[4,128,768]{2,1,0:T(8,128)(2,1)}, u32[]{:S(2)}, u32[]{:S(2)}) async-start(bf16[4,128,768]{2,1,0:T(8,128)(2,1)} %convert_element_type.127), calls=%async_computation.11 | async-start | bytes 1572864 | tf_op jit(solution)/shard_map/all_to_all | solution.py:335
  877.4 4.8 copy-start.6
  877.5 4.8 copy-start.7
  878.4 6.9 copy-start.17
  878.4 13.3 %all-to-all-start.9 = ((bf16[4,128,768]{2,1,0:T(8,128)(2,1)}), bf16[4,128,768]{2,1,0:T(8,128)(2,1)S(1)}, u32[]{:S(2)}, u32[]{:S(2)}) async-start(bf16[4,128,768]{2,1,0:T(8,128)(2,1)} %convert_element_type.123), calls=%async_computation.9 | async-start | bytes 1572864 | tf_op jit(solution)/shard_map/all_to_all | solution.py:334
Sparse Core Ops, SparseCore 0:
  691.4 88.1 all-reduce.3
  797.1 66.2 all-reduce.5
where the time goes:
time: 910 us; the launch traced here: 900 us
  waiting for transfers between devices  253 us (28%)
  local copies, waits for them, and re-layouts  228 us (25%)
  blocking collectives  148 us (16%)
  other arithmetic  108 us (12%)
  matrix products  94.3 us (10%)
  starting transfers between devices  53.7 us (6%)
  between operations  15 us (2%)
    pmax x1, blocking collectives, body(): lax.pmax(jnp.max(video_scores, axis=-1), 'seq')  104 us
    reshape x4, local copies, waits for them, and re-layouts, spread_grads(): grad_blk[:, :KT * TILE].reshape(block_tiles, KT, TILE, pool_total.shape[2])  68.1 us
    all_to_all x1, waiting for transfers between devices, body(): lax.all_to_all(send_keys, 'seq', split_axis=0, concat_axis=0, tiled=True)  67.4 us
    all_to_all x1, waiting for transfers between devices, body(): lax.all_to_all(send_values, 'seq', split_axis=0, concat_axis=0, tiled=True)  66.3 us
    scatter-add x2, other arithmetic, spread_grads(): pool_total.at[pool_slot].add(tile_part)  60.2 us
    reshape x4, local copies, waits for them, and re-layouts, block_rows(): picked = pool[slot_blk].reshape(block_tiles, KT * TILE, head_count, HD)  46.3 us
    psum x1, blocking collectives, body(): lax.psum((jnp.sum(video_exp, axis=-1), split_product('htk,khd->thd', vide...  44.6 us
    all_to_all x1, waiting for transfers between devices, body(): lax.all_to_all(value_acc[shard_tiles:].reshape(groups, MOST * TILE, featu...  43.1 us
  transfers between devices with their start and end apart: 14, of which 7 were waited for; matrix products, arithmetic and copies ran while one was open for 47% of the time, Pallas kernels for 0%

commit v1 on v0

v1 whole, which is shorter than its diff:
```python
import functools

import jax
import jax.numpy as jnp
from jax import lax
from jax.experimental import pallas as pl
from jax.experimental.pallas import tpu as pltpu
from jax.sharding import Mesh, PartitionSpec as P

HD = 128
TILE = 128
NEGATIVE = -1e30
LOG2E = 1.4426950408889634
FACTOR = HD**-0.5


def dot_nt(a, b):
    return lax.dot_general(a, b, (((1,), (1,)), ((), ())), preferred_element_type=jnp.float32)


def dot_tn(a, b):
    return lax.dot_general(a, b, (((0,), (0,)), ((), ())), preferred_element_type=jnp.float32)


def dot_nn(a, b):
    return lax.dot_general(a, b, (((1,), (0,)), ((), ())), preferred_element_type=jnp.float32)


def attend_kernel(
    outer,
    entries,
    slot_ref,
    count_ref,
    q_ref,
    g_ref,
    k_ref,
    v_ref,
    tq_ref,
    tg_ref,
    tk_ref,
    tv_ref,
    bias_ref,
    o_ref,
    dq_ref,
    dk_ref,
    dv_ref,
    to_ref,
    tdq_ref,
    kbuf,
    vbuf,
    sbuf,
    dk_acc,
    dv_acc,
):
    video = k_ref.shape[0]
    text = tk_ref.shape[0]
    chunk = q_ref.shape[0]
    part = tq_ref.shape[0]
    listed = entries * TILE
    scale2 = FACTOR * LOG2E
    kbuf[pl.ds(listed, text), :] = tk_ref[...]
    vbuf[pl.ds(listed, text), :] = tv_ref[...]

    block = 512
    steps = video // block
    tq = tq_ref[...]
    tg = tg_ref[...]
    text_s = dot_nt(tk_ref[...], tq) * scale2 + bias_ref[:, :part]
    top = jnp.max(text_s, axis=0, keepdims=True)

    def scores(i, top):
        rows = pl.ds(pl.multiple_of(i * block, block), block)
        s = dot_nt(k_ref[rows, :], tq) * scale2
        sbuf[rows, :] = s
        return jnp.maximum(top, jnp.max(s, axis=0, keepdims=True))

    top = lax.fori_loop(0, steps, scores, top)
    text_e = jnp.exp2(text_s - top)

    def weigh(i, carry):
        total, out = carry
        rows = pl.ds(pl.multiple_of(i * block, block), block)
        e = jnp.exp2(sbuf[rows, :] - top)
        sbuf[rows, :] = e
        out = out + dot_tn(e.astype(jnp.bfloat16), v_ref[rows, :])
        return total + jnp.sum(e, axis=0, keepdims=True), out

    total, out = lax.fori_loop(
        0,
        steps,
        weigh,
        (
            jnp.sum(text_e, axis=0, keepdims=True),
            dot_tn(text_e.astype(jnp.bfloat16), tv_ref[...]),
        ),
    )
    inverse = 1.0 / total
    out = out * jnp.transpose(inverse)
    to_ref[...] = out.astype(jnp.bfloat16)
    delta = jnp.transpose(jnp.sum(tg.astype(jnp.float32) * out, axis=1, keepdims=True))

    def spread(e, key, value):
        p = e * inverse
        dv = dot_nn(p.astype(jnp.bfloat16), tg)
        ds = (p * (dot_nt(value, tg) - delta)).astype(jnp.bfloat16)
        return dot_nn(ds, tq), dv, dot_tn(ds, key)

    dk, dv, dq = spread(text_e, tk_ref[...], tv_ref[...])
    dk_acc[pl.ds(video, text), :] = dk
    dv_acc[pl.ds(video, text), :] = dv

    def back(i, dq):
        rows = pl.ds(pl.multiple_of(i * block, block), block)
        dk, dv, more = spread(sbuf[rows, :], k_ref[rows, :], v_ref[rows, :])
        dk_acc[rows, :] = dk
        dv_acc[rows, :] = dv
        return dq + more

    dq = lax.fori_loop(0, steps, back, dq)
    tdq_ref[...] = (dq * FACTOR).astype(jnp.bfloat16)

    def tile(i, carry):
        rows = pl.ds(pl.multiple_of(i * TILE, TILE), TILE)
        spots = [
            pl.ds(pl.multiple_of(slot_ref[i * entries + e] * TILE, TILE), TILE)
            for e in range(entries)
        ]
        count = count_ref[i]
        q = q_ref[rows, :]
        g = g_ref[rows, :]
        for e in range(entries):
            kbuf[pl.ds(e * TILE, TILE), :] = k_ref[spots[e], :]
            vbuf[pl.ds(e * TILE, TILE), :] = v_ref[spots[e], :]
        keys = kbuf[...]
        values = vbuf[...]
        s = dot_nt(keys, q) * scale2
        parts = [
            s[e * TILE : (e + 1) * TILE] + jnp.where(e < count, 0.0, NEGATIVE)
            for e in range(entries)
        ]
        s = jnp.concatenate(parts + [s[listed:] + bias_ref[...]], axis=0)
        e = jnp.exp2(s - jnp.max(s, axis=0, keepdims=True))
        p = e * (1.0 / jnp.sum(e, axis=0, keepdims=True))
        weights = p.astype(jnp.bfloat16)
        out = dot_tn(weights, values)
        o_ref[rows, :] = out.astype(jnp.bfloat16)
        delta = jnp.transpose(jnp.sum(g.astype(jnp.float32) * out, axis=1, keepdims=True))
        ds = (p * (dot_nt(values, g) - delta)).astype(jnp.bfloat16)
        dq_ref[rows, :] = (dot_tn(ds, keys) * FACTOR).astype(jnp.bfloat16)
        dk = dot_nn(ds, q)
        dv = dot_nn(weights, g)
        for e in range(entries):
            dk_acc[spots[e], :] += dk[e * TILE : (e + 1) * TILE]
            dv_acc[spots[e], :] += dv[e * TILE : (e + 1) * TILE]
        dk_acc[pl.ds(video, text), :] += dk[listed:]
        dv_acc[pl.ds(video, text), :] += dv[listed:]
        return carry

    lax.fori_loop(0, chunk // TILE, tile, 0)

    for z in range(outer):
        at = z * (chunk + part)
        dk_ref[pl.ds(at, chunk), :] = (dk_acc[pl.ds(z * chunk, chunk), :] * FACTOR).astype(
            dk_ref.dtype
        )
        dv_ref[pl.ds(at, chunk), :] = dv_acc[pl.ds(z * chunk, chunk), :].astype(dv_ref.dtype)
        dk_ref[pl.ds(at + chunk, part), :] = (
            dk_acc[pl.ds(video + z * part, part), :] * FACTOR
        ).astype(dk_ref.dtype)
        dv_ref[pl.ds(at + chunk, part), :] = dv_acc[pl.ds(video + z * part, part), :].astype(
            dv_ref.dtype
        )


def attend(outer, slots, counts, q, g, k, v, tq, tg, tk, tv, bias):
    chunk, width = q.shape
    video = k.shape[0]
    text = tk.shape[0]
    part = tq.shape[0]
    entries = slots.shape[1]
    rows = lambda n: pl.BlockSpec((n, HD), lambda h, *_: (0, h))
    total = video + text
    call = pl.pallas_call(
        functools.partial(attend_kernel, outer, entries),
        grid_spec=pltpu.PrefetchScalarGridSpec(
            num_scalar_prefetch=2,
            grid=(width // HD,),
            in_specs=[
                rows(chunk),
                rows(chunk),
                rows(video),
                rows(video),
                rows(part),
                rows(part),
                rows(text),
                rows(text),
                pl.BlockSpec((text, TILE), lambda h, *_: (0, 0)),
            ],
            out_specs=[
                rows(chunk),
                rows(chunk),
                rows(total),
                rows(total),
                rows(part),
                rows(part),
            ],
            scratch_shapes=[
                pltpu.VMEM((entries * TILE + text, HD), jnp.bfloat16),
                pltpu.VMEM((entries * TILE + text, HD), jnp.bfloat16),
                pltpu.VMEM((video, part), jnp.float32),
                pltpu.VMEM((total, HD), jnp.float32),
                pltpu.VMEM((total, HD), jnp.float32),
            ],
        ),
        out_shape=[
            jax.ShapeDtypeStruct((chunk, width), jnp.bfloat16),
            jax.ShapeDtypeStruct((chunk, width), jnp.bfloat16),
            jax.ShapeDtypeStruct((total, width), jnp.bfloat16),
            jax.ShapeDtypeStruct((total, width), jnp.bfloat16),
            jax.ShapeDtypeStruct((part, width), jnp.bfloat16),
            jax.ShapeDtypeStruct((part, width), jnp.bfloat16),
        ],
        compiler_params=pltpu.CompilerParams(vmem_limit_bytes=63 * 1024 * 1024),
        name="attend",
    )
    return call(slots.reshape(-1), counts, q, g, k, v, tq, tg, tk, tv, bias)


def body(
    video_query,
    video_key,
    video_value,
    video_grad,
    text_query,
    text_key,
    text_value,
    text_grad,
    tile_list,
    tile_count,
    text_mask,
):
    outer, core, head = (lax.axis_size(name) for name in ("outer", "core", "head"))
    own, own_core = lax.axis_index("outer"), lax.axis_index("core")
    near = ("head", "core")
    rows, width = video_query.shape
    feat = width // (head * core)
    text = text_query.shape[0]
    part = text // outer
    tiles = rows // TILE

    def to_heads(x):
        return lax.all_to_all(x, near, split_axis=1, concat_axis=0, tiled=True)

    def to_tokens(x):
        return lax.all_to_all(x, near, split_axis=0, concat_axis=1, tiled=True)

    keys = lax.all_gather(to_heads(video_key), "outer", axis=0, tiled=True)
    values = lax.all_gather(to_heads(video_value), "outer", axis=0, tiled=True)
    queries = to_heads(video_query)
    grads = to_heads(video_grad)
    chunk = queries.shape[0]

    block = tile_list // tiles
    spot = ((block // head) % core) + (block % head) * core
    slot = (block // (head * core)) * (chunk // TILE) + spot * tiles + tile_list % tiles
    place = jnp.arange(chunk // TILE)
    mine = place // tiles
    mine = (own * core + mine % core) * head + mine // core
    mine = mine * tiles + place % tiles
    slots = slot[mine].astype(jnp.int32)
    counts = tile_count[mine].astype(jnp.int32)
    bias = jnp.broadcast_to(
        jnp.where(text_mask > 0, 0.0, NEGATIVE).astype(jnp.float32)[:, None], (text, TILE)
    )

    mine_of = lambda x: lax.dynamic_slice_in_dim(x, own_core * feat, feat, 1)
    part_of = lambda x: lax.dynamic_slice_in_dim(x, own * part, part, 0)
    tk, tv, tq, tg = (mine_of(x) for x in (text_key, text_value, text_query, text_grad))
    o, dq, dk, dv, to, tdq = attend(
        outer, slots, counts, queries, grads, keys, values, part_of(tq), part_of(tg), tk, tv, bias
    )
    attended = to_tokens(o)
    query_grad = to_tokens(dq)
    dk = lax.psum_scatter(dk, "outer", scatter_dimension=0, tiled=True)
    dv = lax.psum_scatter(dv, "outer", scatter_dimension=0, tiled=True)
    key_grad = to_tokens(dk[:chunk])
    value_grad = to_tokens(dv[:chunk])
    texts = jnp.stack([to, tdq, dk[chunk:], dv[chunk:]])
    texts = lax.all_gather(texts, ("outer", "core"), axis=0, tiled=False)
    texts = texts.reshape(outer, core, 4, part, feat).transpose(2, 0, 3, 1, 4)
    texts = texts.reshape(4, text, core * feat)
    return (attended, query_grad, key_grad, value_grad, texts[0], texts[1], texts[2], texts[3])


def solution(mesh):
    seq, head = mesh.shape["seq"], mesh.shape["head"]
    video = P(("outer", "core", "head"), None)
    side = P(None, "head")

    def run(*arrays):
        heads = arrays[0].shape[1] // HD // head
        core = 2 if heads % 2 == 0 and seq % 2 == 0 else 1
        grid = Mesh(mesh.devices.reshape(seq // core, core, head), ("outer", "core", "head"))
        return jax.shard_map(
            body,
            mesh=grid,
            in_specs=(video,) * 4 + (side,) * 4 + (P(), P(), P()),
            out_specs=(video,) * 4 + (side,) * 4,
            check_vma=False,
        )(*arrays)

    return run
```

time: 910 us -> 412 us (0.45)
  local copies, waits for them, and re-layouts: 228 us -> 25.7 us
  blocking collectives: 148 us -> 33.5 us
  other arithmetic: 108 us -> 0.77 us
  matrix products: 94.3 us -> 0 us
  Pallas kernels: 0 us -> 65.6 us
  starting transfers between devices: 53.7 us -> 22.5 us
    all_to_all x12 -> x6, waiting for transfers between devices: 191 us -> 49 us  [the longest x4 31.5 us: to_tokens(): return lax.all_to_all(x, near, split_axis=0, concat_axis=1, tiled=True)]
    reshape x18 -> x1, local copies, waits for them, and re-layouts: 134 us -> 0.66 us  [attend(): return call(slots.reshape(-1), counts, q, g, k, v, tq, tg, tk, tv, bias)]
    reduce_scatter x0 -> x2, waiting for transfers between devices: none -> 123 us  [the longest x1 64.9 us: body(): dk = lax.psum_scatter(dk, 'outer', scatter_dimension=0, tiled=True)]
    pmax x1 -> x0, blocking collectives: 104 us -> none  [body(): lax.pmax(jnp.max(video_scores, axis=-1), 'seq')]
    dot_general x24 -> x0, matrix products: 94.3 us -> none  [the longest x1 13 us: block_backward(): jnp.einsum('bthd,bkhd->bhtk', grad_blk, value_blk, preferred_element_type...]
    scatter-add x4 -> x0, other arithmetic: 78.6 us -> none  [the longest x2 60.2 us: spread_grads(): pool_total.at[pool_slot].add(tile_part)]
    all_gather x0 -> x3, waiting for transfers between devices: none -> 76.7 us  [the longest x1 63.7 us: body(): values = lax.all_gather(to_heads(video_value), 'outer', axis=0, tiled=True)]
    pallas_call x0 -> x1, Pallas kernels: none -> 65.6 us  [attend(): return call(slots.reshape(-1), counts, q, g, k, v, tq, tg, tk, tv, bias)]
  transfers between devices with their start and end apart: 14 -> 11, of which waited for: 7 -> 9; matrix products, arithmetic and copies ran while one was open for 47% -> 4% of each run, Pallas kernels for 0% -> 0%
where the time goes in v1:
time: 412 us; the launch traced here: 411 us
  waiting for transfers between devices  249 us (60%)
  Pallas kernels  65.6 us (16%)
  blocking collectives  33.5 us (8%)
  local copies, waits for them, and re-layouts  25.7 us (6%)
  starting transfers between devices  22.5 us (5%)
  between operations  14 us (3%)
    pallas_call x1, Pallas kernels, attend(): return call(slots.reshape(-1), counts, q, g, k, v, tq, tg, tk, tv, bias)  65.6 us
    reduce_scatter x1, waiting for transfers between devices, body(): dk = lax.psum_scatter(dk, 'outer', scatter_dimension=0, tiled=True)  64.9 us
    all_gather x1, waiting for transfers between devices, body(): values = lax.all_gather(to_heads(video_value), 'outer', axis=0, tiled=True)  63.7 us
    reduce_scatter x1, waiting for transfers between devices, body(): dv = lax.psum_scatter(dv, 'outer', scatter_dimension=0, tiled=True)  57.9 us
    all_to_all x2, blocking collectives, to_heads(): return lax.all_to_all(x, near, split_axis=1, concat_axis=0, tiled=True)  33.5 us
    all_to_all x4, waiting for transfers between devices, to_tokens(): return lax.all_to_all(x, near, split_axis=0, concat_axis=1, tiled=True)  31.5 us
    all_to_all x2, waiting for transfers between devices, to_heads(): return lax.all_to_all(x, near, split_axis=1, concat_axis=0, tiled=True)  17.5 us
    all_to_all x4, starting transfers between devices, to_tokens(): return lax.all_to_all(x, near, split_axis=0, concat_axis=1, tiled=True)  14.4 us
  transfers between devices with their start and end apart: 11, of which 9 were waited for; matrix products, arithmetic and copies ran while one was open for 4% of the time, Pallas kernels for 0%

profile of v1, /device:TPU:0, one launch (start us, length us, event | category | flops | bytes accessed | tf_op | source)
XLA Modules:
  0.0 411.2 jit_solution(16121871965950130688)
XLA Ops:
  7.2 0.0 copy-start
  7.2 0.0 all-gather.5.cloned.1.call-start
  7.2 1.3 copy.84
  8.5 0.0 copy-start.4
  8.5 17.8 %all_to_all.152 = bf16[128,8,384]{2,0,1:T(8,128)(2,1)} all-to-all(bf16[128,8,384]{2,0,1:T(8,128)(2,1)S(1)} %bitcast.74), channel_id=1, replica_groups=mesh['outer'=4,'core'=2,'head'=4] {'head','core'}, dimensions={1} | all-to-all | bytes 1572864 | tf_op jit(solution)/shard_map/all_to_all | solution.py:252
  26.3 0.0 all-gather.5.cloned.1.call-update
  26.3 0.0 all-gather.7.cloned.1.call-start
  26.4 0.1 copy.83
  26.5 0.0 copy-start.5
  26.5 15.8 %all_to_all.153 = bf16[128,8,384]{2,0,1:T(8,128)(2,1)} all-to-all(bf16[128,8,384]{2,0,1:T(8,128)(2,1)S(1)} %bitcast.75), channel_id=1, replica_groups=mesh['outer'=4,'core'=2,'head'=4] {'head','core'}, dimensions={1} | all-to-all | bytes 1572864 | tf_op jit(solution)/shard_map/all_to_all | solution.py:252
  42.2 0.0 all-gather.7.cloned.1.call-update
  42.3 0.0 copy-start.10
  42.3 1.0 copy.86
  43.3 3.7 all-to-all-start
  47.0 1.0 copy.85
  47.9 11.5 %all-to-all-done = bf16[128,8,384]{2,0,1:T(8,128)(2,1)S(1)} async-done(((bf16[128,8,384]{2,0,1:T(8,128)(2,1)}), bf16[128,8,384]{2,0,1:T(8,128)(2,1)S(1)}, u32[]{:S(2)}, u32[]{:S(2)}) %all-to-all-start) | async-done | bytes 786464 | tf_op jit(solution)/shard_map/all_to_all | solution.py:252
  59.5 4.2 %all-to-all-start.1 = ((bf16[128,8,384]{2,0,1:T(8,128)(2,1)}), bf16[128,8,384]{2,0,1:T(8,128)(2,1)}, u32[]{:S(2)}, u32[]{:S(2)}) async-start(bf16[128,8,384]{2,0,1:T(8,128)(2,1)} %bitcast.65), calls=%async_computation.1 | async-start | bytes 1572864 | tf_op jit(solution)/shard_map/all_to_all | solution.py:252
  63.7 0.0 reduce-scatter.5.cloned.1.call-start
  63.8 0.1 copy.51
  63.9 1.2 gather_fusion.1
  65.1 0.6 gather_fusion
  65.7 0.7 reshape.123.slot_ref
  66.3 1.6 dynamic_slice.14.tq_ref
  67.9 1.6 dynamic_slice.15.tg_ref
  69.5 0.0 copy-done.7
  69.5 0.8 constant_dynamic-slice_fusion
  70.3 5.9 %all-to-all-done.1 = bf16[128,8,384]{2,0,1:T(8,128)(2,1)} async-done(((bf16[128,8,384]{2,0,1:T(8,128)(2,1)}), bf16[128,8,384]{2,0,1:T(8,128)(2,1)}, u32[]{:S(2)}, u32[]{:S(2)}) %all-to-all-start.1) | async-done | bytes 786464 | tf_op jit(solution)/shard_map/all_to_all | solution.py:252
  76.3 13.0 %all-gather.5.cloned.1.call-done.k_ref = bf16[4096,384]{1,0:T(8,128)(2,1)} async-done(((bf16[1024,384]{1,0:T(8,128)(2,1)}), bf16[4096,384]{1,0:T(8,128)(2,1)}) %all-gather.5.cloned.1.call-update) | async-done | bytes 3145744 | tf_op jit(solution)/shard_map/all_gather | solution.py:257
  89.3 63.7 %all-gather.7.cloned.1.call-done.v_ref = bf16[4096,384]{1,0:T(8,128)(2,1)} async-done(((bf16[1024,384]{1,0:T(8,128)(2,1)}), bf16[4096,384]{1,0:T(8,128)(2,1)}) %all-gather.7.cloned.1.call-update) | async-done | bytes 3145744 | tf_op jit(solution)/shard_map/all_gather | solution.py:258
  153.0 0.8 broadcast_in_dim.18.bias_ref
  153.7 65.6 %attend.1 = (bf16[1024,384]{1,0:T(8,128)(2,1)}, bf16[1024,384]{1,0:T(8,128)(2,1)}, bf16[4352,384]{1,0:T(8,128)(2,1)}, bf16[4352,384]{1,0:T(8,128)(2,1)}, bf16[64...) custom-call(s32[64]{0:T(128)} %reshape.123.slot_ref, s32[8]{0:T(128)} %gather_fusion.1, bf16[1024,384]{1,0:T(8,128)(2,1)} %bitcast.67, ...), custom_call_target="tpu_custom_call" | custom-call | tf_op jit(solution)/shard_map/attend/pallas_call | solution.py:226
  219.4 0.0 reduce-scatter.5.cloned.1.call-update
  219.4 0.0 reduce-scatter.3.cloned.1.call-start
  219.4 0.5 reduce-scatter.3.cloned.1.call-update
  220.0 3.7 all-to-all-start.5
  223.6 0.0 all-gather.9.cloned.1.call-start
  223.7 57.9 %reduce-scatter.5.cloned.1.call-done = bf16[1088,384]{1,0:T(8,128)(2,1)} async-done(((bf16[4352,384]{1,0:T(8,128)(2,1)}), bf16[1088,384]{1,0:T(8,128)(2,1)}) %reduce-scatter.5.cloned.1.call-update) | async-done | bytes 835600 | tf_op jit(solution)/shard_map/reduce_scatter | solution.py:285
  281.6 0.8 slice_bitcast_fusion
  282.4 64.9 %reduce-scatter.3.cloned.1.call-done = bf16[1088,384]{1,0:T(8,128)(2,1)} async-done(((bf16[4352,384]{1,0:T(8,128)(2,1)}), bf16[1088,384]{1,0:T(8,128)(2,1)}) %reduce-scatter.3.cloned.1.call-update) | async-done | bytes 835600 | tf_op jit(solution)/shard_map/reduce_scatter | solution.py:284
  347.3 0.9 slice_bitcast_fusion.1
  348.2 0.7 pad_maximum_fusion
  348.9 0.0 all-gather.9.cloned.1.call-update
  349.0 0.0 all-to-all-done.5
  349.0 3.7 all-to-all-start.4
  352.6 2.1 slice.41
  354.7 10.5 %all-to-all-done.4 = bf16[8,128,384]{2,1,0:T(8,128)(2,1)S(1)} async-done(((bf16[8,128,384]{2,1,0:T(8,128)(2,1)}), bf16[8,128,384]{2,1,0:T(8,128)(2,1)S(1)}, u32[]{:S(2)}, u32[]{:S(2)}) %all-to-all-start.4) | async-done | bytes 786464 | tf_op jit(solution)/shard_map/all_to_all | solution.py:255
  365.2 3.5 all-to-all-start.7
  368.8 1.0 slice.40
  369.7 11.5 %all-to-all-done.7 = bf16[8,128,384]{2,1,0:T(8,128)(2,1)S(1)} async-done(((bf16[8,128,384]{2,1,0:T(8,128)(2,1)}), bf16[8,128,384]{2,1,0:T(8,128)(2,1)S(1)}, u32[]{:S(2)}, u32[]{:S(2)}) %all-to-all-start.7) | async-done | bytes 786464 | tf_op jit(solution)/shard_map/all_to_all | solution.py:255
  381.3 3.5 all-to-all-start.6
  384.8 1.0 copy.72
  385.8 1.0 copy.71
  386.8 1.0 copy.74
  387.8 9.5 %all-to-all-done.6 = bf16[8,128,384]{2,1,0:T(8,128)(2,1)S(1)} async-done(((bf16[8,128,384]{2,1,0:T(8,128)(2,1)}), bf16[8,128,384]{2,1,0:T(8,128)(2,1)S(1)}, u32[]{:S(2)}, u32[]{:S(2)}) %all-to-all-start.6) | async-done | bytes 786464 | tf_op jit(solution)/shard_map/all_to_all | solution.py:255
  397.3 1.0 copy.73
  398.3 1.5 fusion.12
  399.9 0.4 copy.66
  400.3 0.8 copy.78
  401.1 0.4 copy.65
  401.5 0.8 copy.77
  402.3 0.4 copy.64
  402.7 0.8 copy.76
  403.5 0.4 copy.63
  403.9 0.8 copy.75
  (24 shorter events, 0.1 us)
Async XLA Ops:
  7.2 56.7 %copy-start = (s32[32]{0:T(128)S(1)}, s32[32]{0:T(128)}, u32[]{:S(2)}) copy-start(s32[32]{0:T(128)} %param.20) | copy-start | bytes 388
  7.2 19.2 %copy-start.3 = (bf16[128,3072]{1,0:T(8,128)(2,1)S(1)}, bf16[128,3072]{1,0:T(8,128)(2,1)}, u32[]{:S(2)}) copy-start(bf16[128,3072]{1,0:T(8,128)(2,1)} %param.13) | copy-start | bytes 2359300
  7.2 82.1 %all-gather.5.cloned.1.call-start = ((), (), s32[]{:S(2)}) async-start(), calls=%async_computation.10 | async-start | bytes 3932160 | tf_op jit(solution)/shard_map/all_gather | solution.py:257
  8.5 33.7 %copy-start.4 = (bf16[128,3072]{1,0:T(8,128)(2,1)S(1)}, bf16[128,3072]{1,0:T(8,128)(2,1)}, u32[]{:S(2)}) copy-start(bf16[128,3072]{1,0:T(8,128)(2,1)} %param.11) | copy-start | bytes 2359300
  26.3 126.6 %all-gather.7.cloned.1.call-start = ((), (), s32[]{:S(2)}) async-start(), calls=%async_computation.11 | async-start | bytes 3932160 | tf_op jit(solution)/shard_map/all_gather | solution.py:258
  26.5 20.5 %copy-start.5 = (bf16[128,3072]{1,0:T(8,128)(2,1)S(1)}, bf16[128,3072]{1,0:T(8,128)(2,1)}, u32[]{:S(2)}) copy-start(bf16[128,3072]{1,0:T(8,128)(2,1)} %param.14) | copy-start | bytes 2359300
  42.3 21.5 %copy-start.10 = (s32[32,8]{0,1:T(8,128)S(1)}, s32[32,8]{0,1:T(8,128)}, u32[]{:S(2)}) copy-start(s32[32,8]{0,1:T(8,128)} %param.19) | copy-start | bytes 3076
  43.3 26.3 %copy-start.6 = (bf16[256,768]{1,0:T(8,128)(2,1)S(1)}, bf16[256,768]{1,0:T(8,128)(2,1)}, u32[]{:S(2)}) copy-start(bf16[256,768]{1,0:T(8,128)(2,1)} %param.17) | copy-start | bytes 1179652
  43.3 26.3 %copy-start.7 = (bf16[256,768]{1,0:T(8,128)(2,1)S(1)}, bf16[256,768]{1,0:T(8,128)(2,1)}, u32[]{:S(2)}) copy-start(bf16[256,768]{1,0:T(8,128)(2,1)} %param.16) | copy-start | bytes 1179652
  43.3 27.1 %copy-start.11 = (s32[256]{0:T(256)S(1)}, s32[256]{0:T(256)}, u32[]{:S(2)}) copy-start(s32[256]{0:T(256)} %param.21) | copy-start | bytes 3076
  43.3 16.2 %all-to-all-start = ((bf16[128,8,384]{2,0,1:T(8,128)(2,1)}), bf16[128,8,384]{2,0,1:T(8,128)(2,1)S(1)}, u32[]{:S(2)}, u32[]{:S(2)}) async-start(bf16[128,8,384]{2,0,1:T(8,128)(2,1)} %bitcast.66), calls=%async_computation | async-start | bytes 1572864 | tf_op jit(solution)/shard_map/all_to_all | solution.py:252
  59.5 94.3 %copy-start.1 = (bf16[128,8,384]{2,0,1:T(8,128)(2,1)}, bf16[128,8,384]{2,0,1:T(8,128)(2,1)S(1)}, u32[]{:S(2)}) copy-start(bf16[128,8,384]{2,0,1:T(8,128)(2,1)S(1)} %all-to-all-done) | copy-start | bytes 2359300
  59.5 16.8 %all-to-all-start.1 = ((bf16[128,8,384]{2,0,1:T(8,128)(2,1)}), bf16[128,8,384]{2,0,1:T(8,128)(2,1)}, u32[]{:S(2)}, u32[]{:S(2)}) async-start(bf16[128,8,384]{2,0,1:T(8,128)(2,1)} %bitcast.65), calls=%async_computation.1 | async-start | bytes 1572864 | tf_op jit(solution)/shard_map/all_to_all | solution.py:252
  63.7 217.9 %reduce-scatter.5.cloned.1.call-start = ((), (), s32[]{:S(2)}) async-start(), calls=%async_computation.13 | async-start | bytes 4177920 | tf_op jit(solution)/shard_map/reduce_scatter | solution.py:285
  219.4 128.8 %copy-start.8 = (bf16[64,384]{1,0:T(8,128)(2,1)S(1)}, bf16[64,384]{1,0:T(8,128)(2,1)}, u32[]{:S(2)}) copy-start(bf16[64,384]{1,0:T(8,128)(2,1)} %get-tuple-element.18) | copy-start | bytes 147460
  219.4 128.8 %copy-start.9 = (bf16[64,384]{1,0:T(8,128)(2,1)S(1)}, bf16[64,384]{1,0:T(8,128)(2,1)}, u32[]{:S(2)}) copy-start(bf16[64,384]{1,0:T(8,128)(2,1)} %get-tuple-element.19) | copy-start | bytes 147460
  219.4 127.9 %reduce-scatter.3.cloned.1.call-start = ((), (), s32[]{:S(2)}) async-start(), calls=%async_computation.12 | async-start | bytes 4177920 | tf_op jit(solution)/shard_map/reduce_scatter | solution.py:284
  220.0 129.0 %all-to-all-start.5 = ((bf16[8,128,384]{2,1,0:T(8,128)(2,1)}), bf16[8,128,384]{2,1,0:T(8,128)(2,1)S(1)}, u32[]{:S(2)}, u32[]{:S(2)}) async-start(bf16[8,128,384]{2,1,0:T(8,128)(2,1)} %bitcast.11), calls=%async_computation.5 | async-start | bytes 1572864 | tf_op jit(solution)/shard_map/all_to_all | solution.py:255
  223.6 174.7 %all-gather.9.cloned.1.call-start = ((), (), s32[]{:S(2)}) async-start(), calls=%async_computation.14 | async-start | bytes 1769472 | tf_op jit(solution)/shard_map/all_gather | solution.py:289
  347.3 21.4 %copy-start.2 = (bf16[1088,384]{1,0:T(8,128)(2,1)S(1)}, bf16[1088,384]{1,0:T(8,128)(2,1)}, u32[]{:S(2)}) copy-start(bf16[1088,384]{1,0:T(8,128)(2,1)} %reduce-scatter.3.cloned.1.call-done) | copy-start | bytes 2506756
  349.0 16.2 %all-to-all-start.4 = ((bf16[8,128,384]{2,1,0:T(8,128)(2,1)}), bf16[8,128,384]{2,1,0:T(8,128)(2,1)S(1)}, u32[]{:S(2)}, u32[]{:S(2)}) async-start(bf16[8,128,384]{2,1,0:T(8,128)(2,1)} %bitcast.9), calls=%async_computation.4 | async-start | bytes 1572864 | tf_op jit(solution)/shard_map/all_to_all | solution.py:255
  365.2 16.1 %all-to-all-start.7 = ((bf16[8,128,384]{2,1,0:T(8,128)(2,1)}), bf16[8,128,384]{2,1,0:T(8,128)(2,1)S(1)}, u32[]{:S(2)}, u32[]{:S(2)}) async-start(bf16[8,128,384]{2,1,0:T(8,128)(2,1)} %bitcast.15), calls=%async_computation.9 | async-start | bytes 1572864 | tf_op jit(solution)/shard_map/all_to_all | solution.py:255
  381.3 16.1 %all-to-all-start.6 = ((bf16[8,128,384]{2,1,0:T(8,128)(2,1)}), bf16[8,128,384]{2,1,0:T(8,128)(2,1)S(1)}, u32[]{:S(2)}, u32[]{:S(2)}) async-start(bf16[8,128,384]{2,1,0:T(8,128)(2,1)} %bitcast.13), calls=%async_computation.7 | async-start | bytes 1572864 | tf_op jit(solution)/shard_map/all_to_all | solution.py:255
Sparse Core Ops, SparseCore 0:
  26.4 62.7 all-gather.4
  90.8 62.0 all-gather.6
  219.5 62.0 reduce-scatter.4
  283.8 63.4 reduce-scatter.2
  349.4 25.2 all-gather.8

commit v2 on v1

v2 whole, which is shorter than its diff:
```python
import functools

import jax
import jax.numpy as jnp
from jax import lax
from jax.experimental import pallas as pl
from jax.experimental.pallas import tpu as pltpu
from jax.sharding import PartitionSpec as P

HD = 128
TILE = 128
NEGATIVE = -1e30
LOG2E = 1.4426950408889634
FACTOR = HD**-0.5


def dot_nt(a, b):
    return lax.dot_general(a, b, (((1,), (1,)), ((), ())), preferred_element_type=jnp.float32)


def dot_tn(a, b):
    return lax.dot_general(a, b, (((0,), (0,)), ((), ())), preferred_element_type=jnp.float32)


def dot_nn(a, b):
    return lax.dot_general(a, b, (((1,), (0,)), ((), ())), preferred_element_type=jnp.float32)


MESH = pl.DeviceIdType.MESH


def owner_of(index, heads, seq):
    return (index * seq) // heads


def own_head(heads, seq):
    place = lax.axis_index("seq")
    index = (place * heads + seq - 1) // seq
    mine = jnp.logical_and(index < heads, owner_of(index, heads, seq) == place)
    return jnp.minimum(index, heads - 1), mine


def greet(seq, head):
    own_seq, own_group = lax.axis_index("seq"), lax.axis_index("head")
    barrier = pltpu.get_barrier_semaphore()

    def signal(i, carry):
        at = lax.rem(own_seq * head + own_group + i, seq * head)
        pl.semaphore_signal(barrier, inc=1, device_id=(at // head, lax.rem(at, head)), device_id_type=MESH)
        return carry

    lax.fori_loop(1, seq * head, signal, 0)
    pl.semaphore_wait(barrier, seq * head - 1)


def gather_kernel(seq, head, heads, *refs):
    count = 4
    ins, outs = refs[:count], refs[count : 2 * count]
    send_sem, recv_sem, own_sem = refs[2 * count :]
    own_seq, own_group = lax.axis_index("seq"), lax.axis_index("head")
    me = own_seq * head + own_group
    rows = ins[0].shape[0]
    mine_index, mine = own_head(heads, seq)
    greet(seq, head)
    total = head * heads

    def piece(group, index, array):
        column = pl.multiple_of((group * heads + index) * HD, HD)
        return ins[array].at[:, pl.ds(column, HD)]

    def place(device, array):
        return outs[array].at[pl.ds(pl.multiple_of(device * rows, rows), rows), :]

    def remote(group, index, array):
        return pltpu.make_async_remote_copy(
            src_ref=piece(group, index, array),
            dst_ref=place(me, array),
            send_sem=send_sem.at[array, group * heads + index],
            recv_sem=recv_sem.at[array, me],
            device_id=(owner_of(index, heads, seq), group),
            device_id_type=MESH,
        )

    def local(array):
        return pltpu.make_async_copy(
            piece(own_group, mine_index, array), place(me, array), own_sem.at[array]
        )

    def each_target(act):
        def step(i, carry):
            group = lax.rem(own_group + lax.rem(i, head), head)
            index = lax.rem(i // head + own_seq, heads)
            other = jnp.logical_or(group != own_group, owner_of(index, heads, seq) != own_seq)

            @pl.when(other)
            def _():
                for array in range(count):
                    act(remote(group, index, array))

            return carry

        lax.fori_loop(0, total, step, 0)

    each_target(lambda copy: copy.start())

    @pl.when(mine)
    def _():
        for array in range(count):
            local(array).start()

        def arrive(i, carry):
            source = lax.rem(me + i, seq * head)
            for array in range(count):
                pltpu.make_async_remote_copy(
                    src_ref=piece(own_group, mine_index, array),
                    dst_ref=place(source, array),
                    send_sem=send_sem.at[array, 0],
                    recv_sem=recv_sem.at[array, source],
                    device_id=(source // head, lax.rem(source, head)),
                    device_id_type=MESH,
                ).wait_recv()
            return carry

        lax.fori_loop(1, seq * head, arrive, 0)
        for array in range(count):
            local(array).wait()

    each_target(lambda copy: copy.wait_send())


def gather_heads(seq, head, heads, arrays):
    rows = arrays[0].shape[0] * seq * head
    return pl.pallas_call(
        functools.partial(gather_kernel, seq, head, heads),
        in_specs=[pl.BlockSpec(memory_space=pl.ANY)] * 4,
        out_specs=[pl.BlockSpec(memory_space=pl.ANY)] * 4,
        out_shape=[jax.ShapeDtypeStruct((rows, HD), jnp.bfloat16)] * 4,
        scratch_shapes=[
            pltpu.SemaphoreType.DMA((4, head * heads)),
            pltpu.SemaphoreType.DMA((4, seq * head)),
            pltpu.SemaphoreType.DMA((4,)),
        ],
        compiler_params=pltpu.CompilerParams(collective_id=0, has_side_effects=True),
        name="gather_heads",
    )(*arrays)


def scatter_kernel(seq, head, heads, *refs):
    video_in, text_in, video_out, text_out = refs[:4], refs[4:8], refs[8:12], refs[12:16]
    send_sem, recv_sem, own_sem, text_send, text_recv, text_own = refs[16:]
    own_seq, own_group = lax.axis_index("seq"), lax.axis_index("head")
    me = own_seq * head + own_group
    rows = video_out[0].shape[0]
    mine_index, mine = own_head(heads, seq)
    greet(seq, head)

    def part(device, array):
        return video_in[array].at[pl.ds(pl.multiple_of(device * rows, rows), rows), :]

    def column(group, index, array):
        at = pl.multiple_of((group * heads + index) * HD, HD)
        return video_out[array].at[:, pl.ds(at, HD)]

    def text_column(index, array):
        return text_out[array].at[:, pl.ds(pl.multiple_of(index * HD, HD), HD)]

    def remote(device, array):
        return pltpu.make_async_remote_copy(
            src_ref=part(device, array),
            dst_ref=column(own_group, mine_index, array),
            send_sem=send_sem.at[array, device],
            recv_sem=recv_sem.at[array, own_group * heads + mine_index],
            device_id=(device // head, lax.rem(device, head)),
            device_id_type=MESH,
        )

    def text_remote(place, array):
        return pltpu.make_async_remote_copy(
            src_ref=text_in[array],
            dst_ref=text_column(mine_index, array),
            send_sem=text_send.at[array, place],
            recv_sem=text_recv.at[array, mine_index],
            device_id=(place, own_group),
            device_id_type=MESH,
        )

    def local(array):
        return pltpu.make_async_copy(
            part(me, array), column(own_group, mine_index, array), own_sem.at[array]
        )

    def text_local(array):
        return pltpu.make_async_copy(
            text_in[array], text_column(mine_index, array), text_own.at[array]
        )

    def each(act):
        def step(i, carry):
            for array in range(4):
                act(remote(lax.rem(me + i, seq * head), array))
            return carry

        def text_step(i, carry):
            for array in range(4):
                act(text_remote(lax.rem(own_seq + i, seq), array))
            return carry

        lax.fori_loop(1, seq, text_step, 0)
        lax.fori_loop(1, seq * head, step, 0)

    @pl.when(mine)
    def _():
        each(lambda copy: copy.start())
        for array in range(4):
            local(array).start()
            text_local(array).start()

    def arrive(i, carry):
        group = i // heads
        index = lax.rem(i, heads)
        other = jnp.logical_or(group != own_group, owner_of(index, heads, seq) != own_seq)

        @pl.when(other)
        def _():
            for array in range(4):
                pltpu.make_async_remote_copy(
                    src_ref=part(0, array),
                    dst_ref=column(group, index, array),
                    send_sem=send_sem.at[array, 0],
                    recv_sem=recv_sem.at[array, group * heads + index],
                    device_id=(owner_of(index, heads, seq), group),
                    device_id_type=MESH,
                ).wait_recv()

        return carry

    def text_arrive(index, carry):
        @pl.when(owner_of(index, heads, seq) != own_seq)
        def _():
            for array in range(4):
                pltpu.make_async_remote_copy(
                    src_ref=text_in[array],
                    dst_ref=text_column(index, array),
                    send_sem=text_send.at[array, 0],
                    recv_sem=text_recv.at[array, index],
                    device_id=(owner_of(index, heads, seq), own_group),
                    device_id_type=MESH,
                ).wait_recv()

        return carry

    lax.fori_loop(0, head * heads, arrive, 0)
    lax.fori_loop(0, heads, text_arrive, 0)

    @pl.when(mine)
    def _():
        each(lambda copy: copy.wait_send())
        for array in range(4):
            local(array).wait()
            text_local(array).wait()


def scatter_heads(seq, head, heads, video, texts):
    rows = video[0].shape[0] // (seq * head)
    text = texts[0].shape[0]
    return pl.pallas_call(
        functools.partial(scatter_kernel, seq, head, heads),
        in_specs=[pl.BlockSpec(memory_space=pl.ANY)] * 8,
        out_specs=[pl.BlockSpec(memory_space=pl.ANY)] * 8,
        out_shape=[jax.ShapeDtypeStruct((rows, head * heads * HD), jnp.bfloat16)] * 4
        + [jax.ShapeDtypeStruct((text, heads * HD), jnp.bfloat16)] * 4,
        scratch_shapes=[
            pltpu.SemaphoreType.DMA((4, seq * head)),
            pltpu.SemaphoreType.DMA((4, head * heads)),
            pltpu.SemaphoreType.DMA((4,)),
            pltpu.SemaphoreType.DMA((4, seq)),
            pltpu.SemaphoreType.DMA((4, heads)),
            pltpu.SemaphoreType.DMA((4,)),
        ],
        compiler_params=pltpu.CompilerParams(collective_id=1, has_side_effects=True),
        name="scatter_heads",
    )(*video, *texts)


def text_pass(refs):
    (k_ref, v_ref, tq_ref, tg_ref, tk_ref, tv_ref, bias_ref, to_ref, tdq_ref, sbuf, dk_acc, dv_acc) = refs
    video = k_ref.shape[0]
    text = tk_ref.shape[0]
    scale2 = FACTOR * LOG2E
    block = 512
    steps = video // block
    tq = tq_ref[...]
    tg = tg_ref[...]
    text_s = dot_nt(tk_ref[...], tq) * scale2 + bias_ref[:, :1]
    top = jnp.max(text_s, axis=0, keepdims=True)

    def scores(i, top):
        rows = pl.ds(pl.multiple_of(i * block, block), block)
        s = dot_nt(k_ref[rows, :], tq) * scale2
        sbuf[rows, :] = s
        return jnp.maximum(top, jnp.max(s, axis=0, keepdims=True))

    top = lax.fori_loop(0, steps, scores, top)
    text_e = jnp.exp2(text_s - top)

    def weigh(i, carry):
        total, out = carry
        rows = pl.ds(pl.multiple_of(i * block, block), block)
        e = jnp.exp2(sbuf[rows, :] - top)
        sbuf[rows, :] = e
        out = out + dot_tn(e.astype(jnp.bfloat16), v_ref[rows, :])
        return total + jnp.sum(e, axis=0, keepdims=True), out

    total, out = lax.fori_loop(
        0,
        steps,
        weigh,
        (
            jnp.sum(text_e, axis=0, keepdims=True),
            dot_tn(text_e.astype(jnp.bfloat16), tv_ref[...]),
        ),
    )
    inverse = 1.0 / total
    out = out * jnp.transpose(inverse)
    to_ref[...] = out.astype(jnp.bfloat16)
    delta = jnp.transpose(jnp.sum(tg.astype(jnp.float32) * out, axis=1, keepdims=True))

    def spread(e, key, value):
        p = e * inverse
        dv = dot_nn(p.astype(jnp.bfloat16), tg)
        ds = (p * (dot_nt(value, tg) - delta)).astype(jnp.bfloat16)
        return dot_nn(ds, tq), dv, dot_tn(ds, key)

    dk, dv, dq = spread(text_e, tk_ref[...], tv_ref[...])
    dk_acc[pl.ds(video, text), :] = dk
    dv_acc[pl.ds(video, text), :] = dv

    def back(i, dq):
        rows = pl.ds(pl.multiple_of(i * block, block), block)
        dk, dv, more = spread(sbuf[rows, :], k_ref[rows, :], v_ref[rows, :])
        dk_acc[rows, :] = dk
        dv_acc[rows, :] = dv
        return dq + more

    dq = lax.fori_loop(0, steps, back, dq)
    tdq_ref[...] = (dq * FACTOR).astype(jnp.bfloat16)


def attend_kernel(
    entries,
    own_ref,
    slot_ref,
    count_ref,
    q_ref,
    g_ref,
    k_ref,
    v_ref,
    tq_ref,
    tg_ref,
    tk_ref,
    tv_ref,
    bias_ref,
    o_ref,
    dq_ref,
    dk_ref,
    dv_ref,
    to_ref,
    tdq_ref,
    tdk_ref,
    tdv_ref,
    kbuf,
    vbuf,
    sbuf,
    dk_acc,
    dv_acc,
):
    video = k_ref.shape[0]
    text = tk_ref.shape[0]
    chunk = q_ref.shape[0]
    listed = entries * TILE
    scale2 = FACTOR * LOG2E
    step = pl.program_id(0)
    active = own_ref[1] > 0

    @pl.when(jnp.logical_and(active, step == 0))
    def _():
        kbuf[pl.ds(listed, text), :] = tk_ref[...]
        vbuf[pl.ds(listed, text), :] = tv_ref[...]
        text_pass(
            (k_ref, v_ref, tq_ref, tg_ref, tk_ref, tv_ref, bias_ref, to_ref, tdq_ref, sbuf, dk_acc, dv_acc)
        )

    def tile(i, carry):
        rows = pl.ds(pl.multiple_of(i * TILE, TILE), TILE)
        number = step * (chunk // TILE) + i
        spots = [
            pl.ds(pl.multiple_of(slot_ref[number * entries + e] * TILE, TILE), TILE)
            for e in range(entries)
        ]
        count = count_ref[number]
        q = q_ref[rows, :]
        g = g_ref[rows, :]
        for e in range(entries):
            kbuf[pl.ds(e * TILE, TILE), :] = k_ref[spots[e], :]
            vbuf[pl.ds(e * TILE, TILE), :] = v_ref[spots[e], :]
        keys = kbuf[...]
        values = vbuf[...]
        s = dot_nt(keys, q) * scale2
        parts = [
            s[e * TILE : (e + 1) * TILE] + jnp.where(e < count, 0.0, NEGATIVE)
            for e in range(entries)
        ]
        s = jnp.concatenate(parts + [s[listed:] + bias_ref[...]], axis=0)
        e = jnp.exp2(s - jnp.max(s, axis=0, keepdims=True))
        p = e * (1.0 / jnp.sum(e, axis=0, keepdims=True))
        weights = p.astype(jnp.bfloat16)
        out = dot_tn(weights, values)
        o_ref[rows, :] = out.astype(jnp.bfloat16)
        delta = jnp.transpose(jnp.sum(g.astype(jnp.float32) * out, axis=1, keepdims=True))
        ds = (p * (dot_nt(values, g) - delta)).astype(jnp.bfloat16)
        dq_ref[rows, :] = (dot_tn(ds, keys) * FACTOR).astype(jnp.bfloat16)
        dk = dot_nn(ds, q)
        dv = dot_nn(weights, g)
        for e in range(entries):
            dk_acc[spots[e], :] += dk[e * TILE : (e + 1) * TILE]
            dv_acc[spots[e], :] += dv[e * TILE : (e + 1) * TILE]
        dk_acc[pl.ds(video, text), :] += dk[listed:]
        dv_acc[pl.ds(video, text), :] += dv[listed:]
        return carry

    @pl.when(active)
    def _():
        lax.fori_loop(0, chunk // TILE, tile, 0)

    @pl.when(jnp.logical_and(active, step == pl.num_programs(0) - 1))
    def _():
        dk_ref[...] = (dk_acc[pl.ds(0, video), :] * FACTOR).astype(dk_ref.dtype)
        dv_ref[...] = dv_acc[pl.ds(0, video), :].astype(dv_ref.dtype)
        tdk_ref[...] = (dk_acc[pl.ds(video, text), :] * FACTOR).astype(tdk_ref.dtype)
        tdv_ref[...] = dv_acc[pl.ds(video, text), :].astype(tdv_ref.dtype)


def attend(own, slots, counts, q, g, k, v, tq, tg, tk, tv, bias):
    video = k.shape[0]
    text = tk.shape[0]
    entries = slots.shape[1]
    chunk = min(video, 1024)
    total = video + text
    block = pl.BlockSpec((chunk, HD), lambda i, *_: (i, 0))
    held = pl.BlockSpec((video, HD), lambda i, *_: (0, 0), pipeline_mode=pl.Buffered(1))
    given = pl.BlockSpec((text, HD), lambda i, own, *_: (0, own[0]))
    made = pl.BlockSpec((text, HD), lambda i, *_: (0, 0))
    whole = pl.BlockSpec((video, HD), lambda i, *_: (0, 0))
    video_shape = jax.ShapeDtypeStruct((video, HD), jnp.bfloat16)
    text_shape = jax.ShapeDtypeStruct((text, HD), jnp.bfloat16)
    call = pl.pallas_call(
        functools.partial(attend_kernel, entries),
        grid_spec=pltpu.PrefetchScalarGridSpec(
            num_scalar_prefetch=3,
            grid=(video // chunk,),
            in_specs=[block, block, held, held, given, given, given, given, made],
            out_specs=[block, block, whole, whole, made, made, made, made],
            scratch_shapes=[
                pltpu.VMEM((entries * TILE + text, HD), jnp.bfloat16),
                pltpu.VMEM((entries * TILE + text, HD), jnp.bfloat16),
                pltpu.VMEM((video, text), jnp.float32),
                pltpu.VMEM((total, HD), jnp.float32),
                pltpu.VMEM((total, HD), jnp.float32),
            ],
        ),
        out_shape=[video_shape] * 4 + [text_shape] * 4,
        compiler_params=pltpu.CompilerParams(vmem_limit_bytes=63 * 1024 * 1024),
        name="attend",
    )
    return call(own, slots.reshape(-1), counts, q, g, k, v, tq, tg, tk, tv, bias)


def body(
    video_query,
    video_key,
    video_value,
    video_grad,
    text_query,
    text_key,
    text_value,
    text_grad,
    tile_list,
    tile_count,
    text_mask,
):
    seq, head = lax.axis_size("seq"), lax.axis_size("head")
    text, width = text_query.shape
    heads = width // HD
    keys, values, queries, grads = gather_heads(
        seq, head, heads, (video_key, video_value, video_query, video_grad)
    )
    index, mine = own_head(heads, seq)
    own = jnp.stack([index, mine.astype(jnp.int32)]).astype(jnp.int32)
    bias = jnp.broadcast_to(
        jnp.where(text_mask > 0, 0.0, NEGATIVE).astype(jnp.float32)[:, None], (text, HD)
    )
    o, dq, dk, dv, to, tdq, tdk, tdv = attend(
        own,
        tile_list,
        tile_count,
        queries,
        grads,
        keys,
        values,
        text_query,
        text_grad,
        text_key,
        text_value,
        bias,
    )
    return tuple(scatter_heads(seq, head, heads, (o, dq, dk, dv), (to, tdq, tdk, tdv)))


def solution(mesh):
    video = P(("seq", "head"), None)
    side = P(None, "head")
    return jax.shard_map(
        body,
        mesh=mesh,
        in_specs=(video,) * 4 + (side,) * 4 + (P(), P(), P()),
        out_specs=(video,) * 4 + (side,) * 4,
        check_vma=False,
    )
```

time: 412 us -> 275 us (0.67)
  waiting for transfers between devices: 249 us -> 0 us
  Pallas kernels: 65.6 us -> 260 us
  blocking collectives: 33.5 us -> 0 us
  starting transfers between devices: 22.5 us -> 0 us
  local copies, waits for them, and re-layouts: 25.7 us -> 11.9 us
  between operations: 14 us -> 0.73 us
    pallas_call x1 -> x3, Pallas kernels: 65.6 us -> 260 us  [the longest x1 128 us: scatter_heads(): pl.pallas_call(functools.partial(scatter_kernel, seq, head, heads), in_sp...]
    reduce_scatter x2 -> x0, waiting for transfers between devices: 123 us -> none  [the longest x1 64.9 us: body(): dk = lax.psum_scatter(dk, 'outer', scatter_dimension=0, tiled=True)]
    all_gather x3 -> x0, waiting for transfers between devices: 76.7 us -> none  [the longest x1 63.7 us: body(): values = lax.all_gather(to_heads(video_value), 'outer', axis=0, tiled=True)]
    all_to_all x6 -> x0, waiting for transfers between devices: 49 us -> none  [the longest x4 31.5 us: to_tokens(): return lax.all_to_all(x, near, split_axis=0, concat_axis=1, tiled=True)]
    all_to_all x2 -> x0, blocking collectives: 33.5 us -> none  [to_heads(): return lax.all_to_all(x, near, split_axis=1, concat_axis=0, tiled=True)]
    all_to_all x6 -> x0, starting transfers between devices: 22.3 us -> none  [the longest x4 14.4 us: to_tokens(): return lax.all_to_all(x, near, split_axis=0, concat_axis=1, tiled=True)]
    all_to_all x8 -> x0, local copies, waits for them, and re-layouts: 7.31 us -> none  [the longest x4 4.01 us: to_tokens(): return lax.all_to_all(x, near, split_axis=0, concat_axis=1, tiled=True)]
    unnamed x29 -> x27, local copies, waits for them, and re-layouts: 3.32 us -> 10.5 us
  transfers between devices with their start and end apart: 11 -> 0, of which waited for: 9 -> 0; matrix products, arithmetic and copies ran while one was open for 4% -> 0% of each run, Pallas kernels for 0% -> 0%
where the time goes in v2:
time: 275 us; the launch traced here: 273 us
  Pallas kernels  260 us (95%)
  local copies, waits for them, and re-layouts  11.9 us (4%)
    pallas_call x1, Pallas kernels, scatter_heads(): pl.pallas_call(functools.partial(scatter_kernel, seq, head, heads), in_sp...  128 us
    pallas_call x1, Pallas kernels, gather_heads(): pl.pallas_call(functools.partial(gather_kernel, seq, head, heads), in_spe...  67.1 us
    pallas_call x1, Pallas kernels, attend(): call(own, slots.reshape(-1), counts, q, g, k, v, tq, tg, tk, tv, bias)  64.4 us
    unnamed x27, local copies, waits for them, and re-layouts  10.5 us

profile of v2, /device:TPU:0, one launch (start us, length us, event | category | flops | bytes accessed | tf_op | source)
XLA Modules:
  0.0 272.8 jit_solution(16618819937534449043)
XLA Ops:
  0.7 0.0 copy-start.7
  0.7 0.0 copy-start.8
  0.7 0.6 pad_add_fusion.own_ref
  1.3 0.1 copy-done.8
  1.4 0.0 copy-done.7
  1.4 0.1 copy.19
  1.4 0.7 reshape.20.slot_ref
  2.1 0.8 broadcast_in_dim.16.bias_ref
  2.9 67.1 %gather_heads.1 = (bf16[4096,128]{1,0:T(8,128)(2,1)}, bf16[4096,128]{1,0:T(8,128)(2,1)}, bf16[4096,128]{1,0:T(8,128)(2,1)}, bf16[4096,128]{1,0:T(8,128)(2,1)}) custom-call(bf16[128,3072]{1,0:T(8,128)(2,1)} %refs_0_.1, bf16[128,3072]{1,0:T(8,128)(2,1)} %refs_1_.1, bf16[128,3072]{1,0:T(8,128)(2,1)} %refs_2_.1, bf16[128,3072]{1,0:T(8,128)(2,1)} %refs_3_.1), custom_call_target="tpu_custom_call" | custom-call | tf_op jit(solution)/shard_map/gather_heads/pallas_call | solution.py:133
  70.0 64.4 %attend.1 = (bf16[4096,128]{1,0:T(8,128)(2,1)}, bf16[4096,128]{1,0:T(8,128)(2,1)}, bf16[4096,128]{1,0:T(8,128)(2,1)}, bf16[4096,128]{1,0:T(8,128)(2,1)}, bf16[25...) custom-call(s32[2]{0:T(128)} %pad_add_fusion.own_ref, ...), custom_call_target="tpu_custom_call" | custom-call | tf_op jit(solution)/shard_map/attend/pallas_call | solution.py:475
  134.4 128.1 %scatter_heads.1 = (bf16[128,3072]{1,0:T(8,128)(2,1)}, bf16[128,3072]{1,0:T(8,128)(2,1)}, bf16[128,3072]{1,0:T(8,128)(2,1)}, bf16[128,3072]{1,0:T(8,128)(2,1)}, ...) custom-call(bf16[4096,128]{1,0:T(8,128)(2,1)} %get-tuple-element.24.re, ...), custom_call_target="tpu_custom_call" | custom-call | tf_op jit(solution)/shard_map/scatter_heads/pallas_call | solution.py:266
  262.5 0.0 copy-start.2
  262.5 2.1 copy.28
  264.6 0.0 copy-done.2
  264.6 0.0 copy-start.1
  264.6 0.9 copy.29
  265.5 0.5 copy-done.1
  266.0 0.0 copy-start
  266.0 0.9 copy.30
  266.9 0.5 copy-done
  267.5 0.0 copy-start.6
  267.5 0.9 copy.31
  268.3 0.4 copy-done.6
  268.7 0.0 copy-start.5
  268.7 0.7 copy.32
  269.4 0.4 copy-done.5
  269.8 0.0 copy-start.4
  269.8 0.7 copy.33
  270.6 0.4 copy-done.4
  271.0 0.0 copy-start.3
  271.0 0.7 copy.34
  271.7 0.4 copy-done.3
  272.1 0.7 copy.35
  (1 shorter events, 0.0 us)
Async XLA Ops:
  0.7 0.7 copy-start.7
  0.7 0.7 copy-start.8
  262.5 2.1 copy-start.2
  264.6 1.4 copy-start.1
  266.0 1.4 copy-start
  267.5 1.2 copy-start.6
  268.7 1.1 copy-start.5
  269.8 1.1 copy-start.4
  271.0 1.1 copy-start.3

commit v3 on v2

--- a/solution.py
+++ b/solution.py
@@ -152,6 +152,7 @@
     me = own_seq * head + own_group
     rows = video_out[0].shape[0]
     mine_index, mine = own_head(heads, seq)
+    cores = 2 if seq % 2 == 0 else 1
     greet(seq, head)
 
     def part(device, array):
@@ -174,15 +175,31 @@
             device_id_type=MESH,
         )
 
-    def text_remote(place, array):
+    def text_remote(source, index, array, way, place):
         return pltpu.make_async_remote_copy(
-            src_ref=text_in[array],
-            dst_ref=text_column(mine_index, array),
-            send_sem=text_send.at[array, place],
-            recv_sem=text_recv.at[array, mine_index],
+            src_ref=source,
+            dst_ref=text_column(index, array),
+            send_sem=text_send.at[array, index, way],
+            recv_sem=text_recv.at[array, index],
             device_id=(place, own_group),
             device_id_type=MESH,
         )
+
+    def text_sends(act, index, sources):
+        chip, chips = own_seq // cores, seq // cores
+        home = owner_of(index, heads, seq) // cores
+        for way, shift in enumerate((1, -1)):
+            far = chip + shift
+            inside = jnp.logical_and(far >= 0, far < chips)
+
+            @pl.when(jnp.logical_and(inside, (chip - home) * shift >= 0))
+            def _():
+                for array in range(4):
+                    act(text_remote(sources(array), index, array, way, far * cores + own_seq % cores))
+
+        if cores == 2:
+            for array in range(4):
+                act(text_remote(sources(array), index, array, 2, chip * cores + 1 - own_seq % cores))
 
     def local(array):
         return pltpu.make_async_copy(
@@ -200,12 +217,7 @@
                 act(remote(lax.rem(me + i, seq * head), array))
             return carry
 
-        def text_step(i, carry):
-            for array in range(4):
-                act(text_remote(lax.rem(own_seq + i, seq), array))
-            return carry
-
-        lax.fori_loop(1, seq, text_step, 0)
+        text_sends(act, mine_index, lambda array: text_in[array])
         lax.fori_loop(1, seq * head, step, 0)
 
     @pl.when(mine)
@@ -238,19 +250,30 @@
         @pl.when(owner_of(index, heads, seq) != own_seq)
         def _():
             for array in range(4):
-                pltpu.make_async_remote_copy(
-                    src_ref=text_in[array],
-                    dst_ref=text_column(index, array),
-                    send_sem=text_send.at[array, 0],
-                    recv_sem=text_recv.at[array, index],
-                    device_id=(owner_of(index, heads, seq), own_group),
-                    device_id_type=MESH,
-                ).wait_recv()
+                text_remote(text_in[array], index, array, 0, owner_of(index, heads, seq)).wait_recv()
+            pl.when(relays(index))(
+                lambda: text_sends(
+                    lambda copy: copy.start(), index, lambda array: text_column(index, array)
+                )
+            )
 
         return carry
 
+    def relays(index):
+        owner = owner_of(index, heads, seq)
+        return jnp.logical_and(owner != own_seq, owner % cores == own_seq % cores)
+
+    def text_relayed(index, carry):
+        pl.when(relays(index))(
+            lambda: text_sends(
+                lambda copy: copy.wait_send(), index, lambda array: text_column(index, array)
+            )
+        )
+        return carry
+
+    lax.fori_loop(0, heads, text_arrive, 0)
     lax.fori_loop(0, head * heads, arrive, 0)
-    lax.fori_loop(0, heads, text_arrive, 0)
+    lax.fori_loop(0, heads, text_relayed, 0)
 
     @pl.when(mine)
     def _():
@@ -273,7 +296,7 @@
             pltpu.SemaphoreType.DMA((4, seq * head)),
             pltpu.SemaphoreType.DMA((4, head * heads)),
             pltpu.SemaphoreType.DMA((4,)),
-            pltpu.SemaphoreType.DMA((4, seq)),
+            pltpu.SemaphoreType.DMA((4, heads, 3)),
             pltpu.SemaphoreType.DMA((4, heads)),
             pltpu.SemaphoreType.DMA((4,)),
         ],
@@ -377,40 +400,34 @@
     video = k_ref.shape[0]
     text = tk_ref.shape[0]
     chunk = q_ref.shape[0]
-    listed = entries * TILE
     scale2 = FACTOR * LOG2E
     step = pl.program_id(0)
     active = own_ref[1] > 0
 
     @pl.when(jnp.logical_and(active, step == 0))
     def _():
-        kbuf[pl.ds(listed, text), :] = tk_ref[...]
-        vbuf[pl.ds(listed, text), :] = tv_ref[...]
+        kbuf[pl.ds(0, text), :] = tk_ref[...]
+        vbuf[pl.ds(0, text), :] = tv_ref[...]
         text_pass(
             (k_ref, v_ref, tq_ref, tg_ref, tk_ref, tv_ref, bias_ref, to_ref, tdq_ref, sbuf, dk_acc, dv_acc)
         )
 
-    def tile(i, carry):
+    def tile_of(i, used):
         rows = pl.ds(pl.multiple_of(i * TILE, TILE), TILE)
         number = step * (chunk // TILE) + i
         spots = [
             pl.ds(pl.multiple_of(slot_ref[number * entries + e] * TILE, TILE), TILE)
-            for e in range(entries)
+            for e in range(used)
         ]
-        count = count_ref[number]
         q = q_ref[rows, :]
         g = g_ref[rows, :]
-        for e in range(entries):
-            kbuf[pl.ds(e * TILE, TILE), :] = k_ref[spots[e], :]
-            vbuf[pl.ds(e * TILE, TILE), :] = v_ref[spots[e], :]
-        keys = kbuf[...]
-        values = vbuf[...]
+        for e in range(used):
+            kbuf[pl.ds(text + e * TILE, TILE), :] = k_ref[spots[e], :]
+            vbuf[pl.ds(text + e * TILE, TILE), :] = v_ref[spots[e], :]
+        keys = kbuf[pl.ds(0, text + used * TILE), :]
+        values = vbuf[pl.ds(0, text + used * TILE), :]
         s = dot_nt(keys, q) * scale2
-        parts = [
-            s[e * TILE : (e + 1) * TILE] + jnp.where(e < count, 0.0, NEGATIVE)
-            for e in range(entries)
-        ]
-        s = jnp.concatenate(parts + [s[listed:] + bias_ref[...]], axis=0)
+        s = jnp.concatenate([s[:text] + bias_ref[...], s[text:]], axis=0)
         e = jnp.exp2(s - jnp.max(s, axis=0, keepdims=True))
         p = e * (1.0 / jnp.sum(e, axis=0, keepdims=True))
         weights = p.astype(jnp.bfloat16)
@@ -421,11 +438,17 @@
         dq_ref[rows, :] = (dot_tn(ds, keys) * FACTOR).astype(jnp.bfloat16)
         dk = dot_nn(ds, q)
         dv = dot_nn(weights, g)
-        for e in range(entries):
-            dk_acc[spots[e], :] += dk[e * TILE : (e + 1) * TILE]
-            dv_acc[spots[e], :] += dv[e * TILE : (e + 1) * TILE]
-        dk_acc[pl.ds(video, text), :] += dk[listed:]
-        dv_acc[pl.ds(video, text), :] += dv[listed:]
+        for e in range(used):
+            at = text + e * TILE
+            dk_acc[spots[e], :] += dk[at : at + TILE]
+            dv_acc[spots[e], :] += dv[at : at + TILE]
+        dk_acc[pl.ds(video, text), :] += dk[:text]
+        dv_acc[pl.ds(video, text), :] += dv[:text]
+
+    def tile(i, carry):
+        count = count_ref[step * (chunk // TILE) + i]
+        for used in range(1, entries + 1):
+            pl.when(count == used)(functools.partial(tile_of, i, used))
         return carry
 
     @pl.when(active)

time: 275 us -> 257 us (0.935)
  the two profiles are of different devices: /device:TPU:0 before, /device:TPU:7 now
where the time goes in v3:
time: 257 us; the launch traced here: 255 us
  Pallas kernels  242 us (94%)
  local copies, waits for them, and re-layouts  11.9 us (5%)
    pallas_call x1, Pallas kernels, scatter_heads(): pl.pallas_call(functools.partial(scatter_kernel, seq, head, heads), in_sp...  106 us
    pallas_call x1, Pallas kernels, gather_heads(): pl.pallas_call(functools.partial(gather_kernel, seq, head, heads), in_spe...  77.9 us
    pallas_call x1, Pallas kernels, attend(): call(own, slots.reshape(-1), counts, q, g, k, v, tq, tg, tk, tv, bias)  58.5 us
    unnamed x27, local copies, waits for them, and re-layouts  10.5 us

profile of v3, /device:TPU:7, one launch (start us, length us, event | category | flops | bytes accessed | tf_op | source)
XLA Modules:
  0.0 255.4 jit_solution(6018399787591947501)
XLA Ops:
  0.7 0.0 copy-start.7
  0.7 0.0 copy-start.8
  0.7 0.6 pad_add_fusion.own_ref
  1.3 0.1 copy-done.8
  1.4 0.0 copy-done.7
  1.4 0.1 copy.19
  1.4 0.7 reshape.20.slot_ref
  2.1 0.8 broadcast_in_dim.16.bias_ref
  2.9 77.9 %gather_heads.1 = (bf16[4096,128]{1,0:T(8,128)(2,1)}, bf16[4096,128]{1,0:T(8,128)(2,1)}, bf16[4096,128]{1,0:T(8,128)(2,1)}, bf16[4096,128]{1,0:T(8,128)(2,1)}) custom-call(bf16[128,3072]{1,0:T(8,128)(2,1)} %refs_0_.1, bf16[128,3072]{1,0:T(8,128)(2,1)} %refs_1_.1, bf16[128,3072]{1,0:T(8,128)(2,1)} %refs_2_.1, bf16[128,3072]{1,0:T(8,128)(2,1)} %refs_3_.1), custom_call_target="tpu_custom_call" | custom-call | tf_op jit(solution)/shard_map/gather_heads/pallas_call | solution.py:133
  80.8 58.5 %attend.1 = (bf16[4096,128]{1,0:T(8,128)(2,1)}, bf16[4096,128]{1,0:T(8,128)(2,1)}, bf16[4096,128]{1,0:T(8,128)(2,1)}, bf16[4096,128]{1,0:T(8,128)(2,1)}, bf16[25...) custom-call(s32[2]{0:T(128)} %pad_add_fusion.own_ref, ...), custom_call_target="tpu_custom_call" | custom-call | tf_op jit(solution)/shard_map/attend/pallas_call | solution.py:498
  139.3 105.7 %scatter_heads.1 = (bf16[128,3072]{1,0:T(8,128)(2,1)}, bf16[128,3072]{1,0:T(8,128)(2,1)}, bf16[128,3072]{1,0:T(8,128)(2,1)}, bf16[128,3072]{1,0:T(8,128)(2,1)}, ...) custom-call(bf16[4096,128]{1,0:T(8,128)(2,1)} %get-tuple-element.24.re, ...), custom_call_target="tpu_custom_call" | custom-call | tf_op jit(solution)/shard_map/scatter_heads/pallas_call | solution.py:289
  245.1 0.0 copy-start.2
  245.1 2.1 copy.28
  247.2 0.0 copy-done.2
  247.2 0.0 copy-start.1
  247.2 0.9 copy.29
  248.1 0.5 copy-done.1
  248.6 0.0 copy-start
  248.6 0.9 copy.30
  249.5 0.5 copy-done
  250.0 0.0 copy-start.6
  250.0 0.9 copy.31
  250.9 0.4 copy-done.6
  251.3 0.0 copy-start.5
  251.3 0.7 copy.32
  252.0 0.4 copy-done.5
  252.4 0.0 copy-start.4
  252.4 0.7 copy.33
  253.2 0.4 copy-done.4
  253.6 0.0 copy-start.3
  253.6 0.7 copy.34
  254.3 0.4 copy-done.3
  254.7 0.7 copy.35
  (1 shorter events, 0.0 us)
Async XLA Ops:
  0.7 0.7 copy-start.7
  0.7 0.7 copy-start.8
  245.1 2.1 copy-start.2
  247.2 1.4 copy-start.1
  248.6 1.4 copy-start
  250.0 1.2 copy-start.6
  251.3 1.1 copy-start.5
  252.4 1.1 copy-start.4
  253.6 1.1 copy-start.3

commit v4 on v3

--- a/solution.py
+++ b/solution.py
@@ -175,31 +175,28 @@
             device_id_type=MESH,
         )
 
-    def text_remote(source, index, array, way, place):
+    def text_remote(source, index, array, place):
         return pltpu.make_async_remote_copy(
             src_ref=source,
             dst_ref=text_column(index, array),
-            send_sem=text_send.at[array, index, way],
+            send_sem=text_send.at[array, index, place],
             recv_sem=text_recv.at[array, index],
             device_id=(place, own_group),
             device_id_type=MESH,
         )
 
-    def text_sends(act, index, sources):
-        chip, chips = own_seq // cores, seq // cores
-        home = owner_of(index, heads, seq) // cores
-        for way, shift in enumerate((1, -1)):
-            far = chip + shift
-            inside = jnp.logical_and(far >= 0, far < chips)
-
-            @pl.when(jnp.logical_and(inside, (chip - home) * shift >= 0))
-            def _():
-                for array in range(4):
-                    act(text_remote(sources(array), index, array, way, far * cores + own_seq % cores))
-
+    def text_beside(act, index, sources):
         if cores == 2:
             for array in range(4):
-                act(text_remote(sources(array), index, array, 2, chip * cores + 1 - own_seq % cores))
+                act(text_remote(sources(array), index, array, own_seq + 1 - 2 * (own_seq % 2)))
+
+    def text_far(act, index, sources):
+        def step(i, carry):
+            for array in range(4):
+                act(text_remote(sources(array), index, array, lax.rem(own_seq + i * cores, seq)))
+            return carry
+
+        lax.fori_loop(1, seq // cores, step, 0)
 
     def local(array):
         return pltpu.make_async_copy(
@@ -217,7 +214,8 @@
                 act(remote(lax.rem(me + i, seq * head), array))
             return carry
 
-        text_sends(act, mine_index, lambda array: text_in[array])
+        text_far(act, mine_index, lambda array: text_in[array])
+        text_beside(act, mine_index, lambda array: text_in[array])
         lax.fori_loop(1, seq * head, step, 0)
 
     @pl.when(mine)
@@ -250,9 +248,9 @@
         @pl.when(owner_of(index, heads, seq) != own_seq)
         def _():
             for array in range(4):
-                text_remote(text_in[array], index, array, 0, owner_of(index, heads, seq)).wait_recv()
+                text_remote(text_in[array], index, array, owner_of(index, heads, seq)).wait_recv()
             pl.when(relays(index))(
-                lambda: text_sends(
+                lambda: text_beside(
                     lambda copy: copy.start(), index, lambda array: text_column(index, array)
                 )
             )
@@ -265,7 +263,7 @@
 
     def text_relayed(index, carry):
         pl.when(relays(index))(
-            lambda: text_sends(
+            lambda: text_beside(
                 lambda copy: copy.wait_send(), index, lambda array: text_column(index, array)
             )
         )
@@ -296,13 +294,31 @@
             pltpu.SemaphoreType.DMA((4, seq * head)),
             pltpu.SemaphoreType.DMA((4, head * heads)),
             pltpu.SemaphoreType.DMA((4,)),
-            pltpu.SemaphoreType.DMA((4, heads, 3)),
+            pltpu.SemaphoreType.DMA((4, heads, seq)),
             pltpu.SemaphoreType.DMA((4, heads)),
             pltpu.SemaphoreType.DMA((4,)),
         ],
         compiler_params=pltpu.CompilerParams(collective_id=1, has_side_effects=True),
         name="scatter_heads",
     )(*video, *texts)
+
+
+def settle_kernel(*refs):
+    for source, result in zip(refs[:8], refs[8:]):
+        result[...] = source[...]
+
+
+def settle(arrays):
+    steps = 4
+    specs = [pl.BlockSpec((x.shape[0] // steps, x.shape[1]), lambda i: (i, 0)) for x in arrays]
+    return pl.pallas_call(
+        settle_kernel,
+        grid=(steps,),
+        in_specs=specs,
+        out_specs=specs,
+        out_shape=[jax.ShapeDtypeStruct(x.shape, x.dtype) for x in arrays],
+        name="settle",
+    )(*arrays)
 
 
 def text_pass(refs):
@@ -431,10 +447,9 @@
         e = jnp.exp2(s - jnp.max(s, axis=0, keepdims=True))
         p = e * (1.0 / jnp.sum(e, axis=0, keepdims=True))
         weights = p.astype(jnp.bfloat16)
-        out = dot_tn(weights, values)
-        o_ref[rows, :] = out.astype(jnp.bfloat16)
-        delta = jnp.transpose(jnp.sum(g.astype(jnp.float32) * out, axis=1, keepdims=True))
-        ds = (p * (dot_nt(values, g) - delta)).astype(jnp.bfloat16)
+        o_ref[rows, :] = dot_tn(weights, values).astype(jnp.bfloat16)
+        pull = p * dot_nt(values, g)
+        ds = (pull - p * jnp.sum(pull, axis=0, keepdims=True)).astype(jnp.bfloat16)
         dq_ref[rows, :] = (dot_tn(ds, keys) * FACTOR).astype(jnp.bfloat16)
         dk = dot_nn(ds, q)
         dv = dot_nn(weights, g)
@@ -536,7 +551,7 @@
         text_value,
         bias,
     )
-    return tuple(scatter_heads(seq, head, heads, (o, dq, dk, dv), (to, tdq, tdk, tdv)))
+    return tuple(settle(scatter_heads(seq, head, heads, (o, dq, dk, dv), (to, tdq, tdk, tdv))))
 
 
 def solution(mesh):

time: 257 us -> 248 us (0.965)
  the two profiles are of different devices: /device:TPU:7 before, /device:TPU:0 now
where the time goes in v4:
time: 248 us; the launch traced here: 247 us
  Pallas kernels  245 us (99%)
    pallas_call x1, Pallas kernels, scatter_heads(): pl.pallas_call(functools.partial(scatter_kernel, seq, head, heads), in_sp...  116 us
    pallas_call x1, Pallas kernels, gather_heads(): pl.pallas_call(functools.partial(gather_kernel, seq, head, heads), in_spe...  67.1 us
    pallas_call x1, Pallas kernels, attend(): call(own, slots.reshape(-1), counts, q, g, k, v, tq, tg, tk, tv, bias)  55.9 us
    pallas_call x1, Pallas kernels, settle(): pl.pallas_call(settle_kernel, grid=(steps,), in_specs=specs, out_specs=sp...  5.07 us

profile of v4, /device:TPU:0, one launch (start us, length us, event | category | flops | bytes accessed | tf_op | source)
XLA Modules:
  0.0 247.4 jit_solution(12749313571908294)
XLA Ops:
  0.7 0.0 copy-start
  0.7 0.0 copy-start.1
  0.7 0.6 pad_add_fusion.own_ref
  1.3 0.1 copy-done.1
  1.4 0.0 copy-done
  1.4 0.1 copy.19
  1.4 0.7 reshape.20.slot_ref
  2.1 0.8 broadcast_in_dim.16.bias_ref
  2.9 67.1 %gather_heads.1 = (bf16[4096,128]{1,0:T(8,128)(2,1)}, bf16[4096,128]{1,0:T(8,128)(2,1)}, bf16[4096,128]{1,0:T(8,128)(2,1)}, bf16[4096,128]{1,0:T(8,128)(2,1)}) custom-call(bf16[128,3072]{1,0:T(8,128)(2,1)} %refs_0_.1, bf16[128,3072]{1,0:T(8,128)(2,1)} %refs_1_.1, bf16[128,3072]{1,0:T(8,128)(2,1)} %refs_2_.1, bf16[128,3072]{1,0:T(8,128)(2,1)} %refs_3_.1), custom_call_target="tpu_custom_call" | custom-call | tf_op jit(solution)/shard_map/gather_heads/pallas_call | solution.py:133
  70.0 55.9 %attend.1 = (bf16[4096,128]{1,0:T(8,128)(2,1)}, bf16[4096,128]{1,0:T(8,128)(2,1)}, bf16[4096,128]{1,0:T(8,128)(2,1)}, bf16[4096,128]{1,0:T(8,128)(2,1)}, bf16[25...) custom-call(s32[2]{0:T(128)} %pad_add_fusion.own_ref, ...), custom_call_target="tpu_custom_call" | custom-call | tf_op jit(solution)/shard_map/attend/pallas_call | solution.py:513
  125.9 116.5 %scatter_heads.1 = (bf16[128,3072]{1,0:T(8,128)(2,1)}, bf16[128,3072]{1,0:T(8,128)(2,1)}, bf16[128,3072]{1,0:T(8,128)(2,1)}, bf16[128,3072]{1,0:T(8,128)(2,1)}, ...) custom-call(bf16[4096,128]{1,0:T(8,128)(2,1)} %get-tuple-element.32.re, ...), custom_call_target="tpu_custom_call" | custom-call | tf_op jit(solution)/shard_map/scatter_heads/pallas_call | solution.py:287
  242.3 5.1 %settle.1 = (bf16[128,3072]{1,0:T(8,128)(2,1)}, bf16[128,3072]{1,0:T(8,128)(2,1)}, bf16[128,3072]{1,0:T(8,128)(2,1)}, bf16[128,3072]{1,0:T(8,128)(2,1)}, bf16[25...) custom-call(bf16[128,3072]{1,0:T(8,128)(2,1)} %get-tuple-element.40.refs_0_, ...), custom_call_target="tpu_custom_call" | custom-call | tf_op jit(solution)/shard_map/settle/pallas_call | solution.py:314
  (1 shorter events, 0.0 us)
Async XLA Ops:
  0.7 0.7 copy-start
  0.7 0.7 copy-start.1

commit v5 on v4

--- a/solution.py
+++ b/solution.py
@@ -211,7 +211,8 @@
     def each(act):
         def step(i, carry):
             for array in range(4):
-                act(remote(lax.rem(me + i, seq * head), array))
+                place = lax.rem(own_seq + i // head, seq)
+                act(remote(place * head + lax.rem(own_group + lax.rem(i, head), head), array))
             return carry
 
         text_far(act, mine_index, lambda array: text_in[array])

time: 248 us -> 240 us (0.968)
  Pallas kernels: 245 us -> 236 us
    pallas_call x1, Pallas kernels: 116 us -> 112 us  [scatter_heads(): pl.pallas_call(functools.partial(scatter_kernel, seq, head, heads), in_sp...]
    pallas_call x1, Pallas kernels: 55.9 us -> 52.3 us  [attend(): call(own, slots.reshape(-1), counts, q, g, k, v, tq, tg, tk, tv, bias)]
where the time goes in v5:
time: 240 us; the launch traced here: 239 us
  Pallas kernels  236 us (98%)
    pallas_call x1, Pallas kernels, scatter_heads(): pl.pallas_call(functools.partial(scatter_kernel, seq, head, heads), in_sp...  112 us
    pallas_call x1, Pallas kernels, gather_heads(): pl.pallas_call(functools.partial(gather_kernel, seq, head, heads), in_spe...  67.1 us
    pallas_call x1, Pallas kernels, attend(): call(own, slots.reshape(-1), counts, q, g, k, v, tq, tg, tk, tv, bias)  52.3 us
    pallas_call x1, Pallas kernels, settle(): pl.pallas_call(settle_kernel, grid=(steps,), in_specs=specs, out_specs=sp...  5.07 us

profile of v5, /device:TPU:0, one launch (start us, length us, event | category | flops | bytes accessed | tf_op | source)
XLA Modules:
  0.0 238.9 jit_solution(15945186314141402232)
XLA Ops:
  0.7 0.0 copy-start
  0.7 0.0 copy-start.1
  0.7 0.6 pad_add_fusion.own_ref
  1.3 0.1 copy-done.1
  1.4 0.0 copy-done
  1.4 0.1 copy.19
  1.4 0.7 reshape.20.slot_ref
  2.1 0.8 broadcast_in_dim.16.bias_ref
  2.9 67.1 %gather_heads.1 = (bf16[4096,128]{1,0:T(8,128)(2,1)}, bf16[4096,128]{1,0:T(8,128)(2,1)}, bf16[4096,128]{1,0:T(8,128)(2,1)}, bf16[4096,128]{1,0:T(8,128)(2,1)}) custom-call(bf16[128,3072]{1,0:T(8,128)(2,1)} %refs_0_.1, bf16[128,3072]{1,0:T(8,128)(2,1)} %refs_1_.1, bf16[128,3072]{1,0:T(8,128)(2,1)} %refs_2_.1, bf16[128,3072]{1,0:T(8,128)(2,1)} %refs_3_.1), custom_call_target="tpu_custom_call" | custom-call | tf_op jit(solution)/shard_map/gather_heads/pallas_call | solution.py:133
  70.0 52.3 %attend.1 = (bf16[4096,128]{1,0:T(8,128)(2,1)}, bf16[4096,128]{1,0:T(8,128)(2,1)}, bf16[4096,128]{1,0:T(8,128)(2,1)}, bf16[4096,128]{1,0:T(8,128)(2,1)}, bf16[25...) custom-call(s32[2]{0:T(128)} %pad_add_fusion.own_ref, ...), custom_call_target="tpu_custom_call" | custom-call | tf_op jit(solution)/shard_map/attend/pallas_call | solution.py:514
  122.3 111.5 %scatter_heads.1 = (bf16[128,3072]{1,0:T(8,128)(2,1)}, bf16[128,3072]{1,0:T(8,128)(2,1)}, bf16[128,3072]{1,0:T(8,128)(2,1)}, bf16[128,3072]{1,0:T(8,128)(2,1)}, ...) custom-call(bf16[4096,128]{1,0:T(8,128)(2,1)} %get-tuple-element.32.re, ...), custom_call_target="tpu_custom_call" | custom-call | tf_op jit(solution)/shard_map/scatter_heads/pallas_call | solution.py:288
  233.8 5.1 %settle.1 = (bf16[128,3072]{1,0:T(8,128)(2,1)}, bf16[128,3072]{1,0:T(8,128)(2,1)}, bf16[128,3072]{1,0:T(8,128)(2,1)}, bf16[128,3072]{1,0:T(8,128)(2,1)}, bf16[25...) custom-call(bf16[128,3072]{1,0:T(8,128)(2,1)} %get-tuple-element.40.refs_0_, ...), custom_call_target="tpu_custom_call" | custom-call | tf_op jit(solution)/shard_map/settle/pallas_call | solution.py:315
  (1 shorter events, 0.0 us)
Async XLA Ops:
  0.7 0.7 copy-start
  0.7 0.7 copy-start.1
